TPU v7x, 32 devices: a whole 2x2x4 slice. The times are simulated.
32 devices in a mesh: seq: 8 (over y, x, core), sub: 4 (over z).
Axes of the slice: x: 2, y: 2, z: 4, core: 2. Of those that a mesh axis runs over, the one named last changes fastest.
Arguments:
- video: bfloat16 [4096, 1536], P(('seq', 'sub')), may hold values from -6 to 6
- conditioning: bfloat16 [5, 1024], replicated, may hold values from -6 to 6
- captions: bfloat16 [1280, 4096], P('sub'), may hold values from -6 to 6
- clip_lengths: int32 [5], replicated, may hold values from 1 to 2048, 4096 in all
- cap_lengths: int32 [5], replicated, may hold values from 64 to 256, as said below
- positions: int32 [4096, 3], P(('seq', 'sub')), may hold values from 0 to 63
- ada_weight: bfloat16 [1024, 6144], P(('seq', 'sub')), may hold values from -0.1875 to 0.1875
- ada_bias: bfloat16 [6144], P(('seq', 'sub')), may hold values from -3 to 3
- query_weight: bfloat16 [1536, 1536], P(('seq', 'sub')), may hold values from -0.15625 to 0.15625
- key_weight: bfloat16 [1536, 1536], P(('seq', 'sub')), may hold values from -0.15625 to 0.15625
- value_weight: bfloat16 [1536, 1536], P(('seq', 'sub')), may hold values from -0.15625 to 0.15625
- out_weight: bfloat16 [1536, 1536], P(('seq', 'sub')), may hold values from -0.15625 to 0.15625
- text_key_weight: bfloat16 [4096, 1536], P(('seq', 'sub')), may hold values from -0.09375 to 0.09375
- text_value_weight: bfloat16 [4096, 1536], P(('seq', 'sub')), may hold values from -0.09375 to 0.09375
- gate_weight: bfloat16 [1536, 4096], P(('seq', 'sub')), may hold values from -0.15625 to 0.15625
- up_weight: bfloat16 [1536, 4096], P(('seq', 'sub')), may hold values from -0.15625 to 0.15625
- down_weight: bfloat16 [4096, 1536], P(('seq', 'sub')), may hold values from -0.09375 to 0.09375
- attn_gain: bfloat16 [1536], P(('seq', 'sub')), may hold values from 0.5 to 1.5
- query_gain: bfloat16 [1536], P(('seq', 'sub')), may hold values from 0.5 to 1.5
- key_gain: bfloat16 [1536], P(('seq', 'sub')), may hold values from 0.5 to 1.5
- text_key_gain: bfloat16 [1536], P(('seq', 'sub')), may hold values from 0.5 to 1.5
- attn_out_gain: bfloat16 [1536], P(('seq', 'sub')), may hold values from 0.5 to 1.5
- ffn_gain: bfloat16 [1536], P(('seq', 'sub')), may hold values from 0.5 to 1.5
- ffn_out_gain: bfloat16 [1536], P(('seq', 'sub')), may hold values from 0.5 to 1.5
- cross_gate: bfloat16 [24], replicated, may hold values from -1.5 to 1.5
- cotangent: bfloat16 [4096, 1536], P(('seq', 'sub')), may hold values from -6 to 6
Outputs:
- block_out: bfloat16 [4096, 1536], P(('seq', 'sub'))
- video_grad: float32 [4096, 1536], P(('seq', 'sub'))
- caption_grad: float32 [1280, 4096], P('sub')
- cond_grad: float32 [5, 1024], replicated
- ada_weight_grad: float32 [1024, 6144], P(('seq', 'sub'))
- ada_bias_grad: float32 [6144], P(('seq', 'sub'))
- query_weight_grad: float32 [1536, 1536], P(('seq', 'sub'))
- key_weight_grad: float32 [1536, 1536], P(('seq', 'sub'))
- value_weight_grad: float32 [1536, 1536], P(('seq', 'sub'))
- out_weight_grad: float32 [1536, 1536], P(('seq', 'sub'))
- text_key_weight_grad: float32 [4096, 1536], P(('seq', 'sub'))
- text_value_weight_grad: float32 [4096, 1536], P(('seq', 'sub'))
- gate_weight_grad: float32 [1536, 4096], P(('seq', 'sub'))
- up_weight_grad: float32 [1536, 4096], P(('seq', 'sub'))
- down_weight_grad: float32 [4096, 1536], P(('seq', 'sub'))
- attn_gain_grad: float32 [1536], P(('seq', 'sub'))
- query_gain_grad: float32 [1536], P(('seq', 'sub'))
- key_gain_grad: float32 [1536], P(('seq', 'sub'))
- text_key_gain_grad: float32 [1536], P(('seq', 'sub'))
- attn_out_gain_grad: float32 [1536], P(('seq', 'sub'))
- ffn_gain_grad: float32 [1536], P(('seq', 'sub'))
- ffn_out_gain_grad: float32 [1536], P(('seq', 'sub'))
- cross_gate_grad: float32 [24], replicated
Inputs may be any that keep to these rules, and one draw needn't show every extreme that they name: `clip_lengths`: clip lengths sum to 4096; the longest clip has exactly 2048 tokens. `cap_lengths`: one clip's caption fills all 256 slots.
All inputs are finite; a program needn't handle non-finite values.
Results may differ from a plain program's by a relative error of at most 0.04.
Values may be sent and summed in bfloat16 or wider, within the bound.
No kernel may reach another device: no remote copies, remote signals or barrier semaphores. Data moves between devices by JAX's collectives and lax.ppermute only.
A program may use at most 384 MiB of HBM per device.

v0:
```python
import math

import jax
import jax.numpy as jnp
from jax import lax
from jax.sharding import PartitionSpec as P

CAP = 256


epsilon = 1e-06
rope_base = 10000.0
masked_score = -1e30
highest = lax.Precision.HIGHEST


def inv_rms(values):
    return lax.rsqrt(jnp.mean(values * values, -1, keepdims=True) + epsilon)


def norm_back(normed_hat, inverse, grad_hat):
    return inverse * (grad_hat - normed_hat * jnp.mean(normed_hat * grad_hat, -1, keepdims=True))


def round_keep(values):
    return lax.optimization_barrier(values.astype(jnp.bfloat16)).astype(jnp.float32)


def rope_tables(positions, head_dim):
    pair_total = head_dim // 2
    frame_pairs = pair_total // 4
    height_pairs = (pair_total - frame_pairs) // 2
    width_pairs = pair_total - frame_pairs - height_pairs
    pieces = []
    for axis_id, pair_count in enumerate((frame_pairs, height_pairs, width_pairs)):
        frequency = rope_base ** (-jnp.arange(pair_count, dtype=jnp.float32) / pair_count)
        pieces.append(positions[:, axis_id].astype(jnp.float32)[:, None] * frequency[None, :])
    angles = jnp.concatenate(pieces, 1)
    return (jnp.cos(angles), jnp.sin(angles))


def rotate(values, cosine, sine):
    shaped = values.reshape(values.shape[0], values.shape[1], -1, 2)
    even_part = shaped[..., 0]
    odd_part = shaped[..., 1]
    cos_part = cosine[:, None, :]
    sin_part = sine[:, None, :]
    turned = jnp.stack(
        [even_part * cos_part - odd_part * sin_part, even_part * sin_part + odd_part * cos_part], -1
    )
    return turned.reshape(values.shape)


def clip_index(token_index, clip_lengths):
    bounds = jnp.cumsum(clip_lengths)
    return jnp.sum((token_index[:, None] >= bounds[None, :]).astype(jnp.int32), 1)


def body(
    video,
    conditioning,
    captions,
    clip_lengths,
    cap_lengths,
    positions,
    ada_weight,
    ada_bias,
    query_weight,
    key_weight,
    value_weight,
    out_weight,
    text_key_weight,
    text_value_weight,
    gate_weight,
    up_weight,
    down_weight,
    attn_gain,
    query_gain,
    key_gain,
    text_key_gain,
    attn_out_gain,
    ffn_gain,
    ffn_out_gain,
    cross_gate,
    cotangent,
):
    num_sub = lax.axis_size("sub")
    num_seq = lax.axis_size("seq")
    tok_rows = video.shape[0]
    model_width = video.shape[1]
    heads_total = cross_gate.shape[0]
    head_dim = model_width // heads_total
    heads_local = heads_total // num_sub
    score_scale = 1.0 / math.sqrt(head_dim)
    device_index = lax.axis_index(("seq", "sub"))
    seq_index = lax.axis_index("seq")
    group_rows = tok_rows * num_sub
    total_tokens = group_rows * num_seq
    clip_count = clip_lengths.shape[0]
    clip_range = jnp.arange(clip_count, dtype=jnp.int32)
    barrier_set = lax.optimization_barrier(
        (
            ada_weight,
            ada_bias,
            query_weight,
            key_weight,
            value_weight,
            out_weight,
            text_key_weight,
            text_value_weight,
            attn_gain,
            query_gain,
            key_gain,
            text_key_gain,
            attn_out_gain,
            video,
        )
    )
    ada_full = lax.all_gather(barrier_set[0], ("seq", "sub"), axis=0, tiled=True)
    ada_bias_full = lax.all_gather(barrier_set[1], ("seq", "sub"), axis=0, tiled=True)
    query_full = lax.all_gather(barrier_set[2], ("seq", "sub"), axis=0, tiled=True)
    key_full = lax.all_gather(barrier_set[3], ("seq", "sub"), axis=0, tiled=True)
    value_full = lax.all_gather(barrier_set[4], ("seq", "sub"), axis=0, tiled=True)
    out_full = lax.all_gather(barrier_set[5], ("seq", "sub"), axis=0, tiled=True)
    text_key_full = lax.all_gather(barrier_set[6], ("seq", "sub"), axis=0, tiled=True)
    text_value_full = lax.all_gather(barrier_set[7], ("seq", "sub"), axis=0, tiled=True)
    attn_gain_full = lax.all_gather(barrier_set[8], ("seq", "sub"), axis=0, tiled=True)
    query_gain_full = lax.all_gather(barrier_set[9], ("seq", "sub"), axis=0, tiled=True)
    key_gain_full = lax.all_gather(barrier_set[10], ("seq", "sub"), axis=0, tiled=True)
    text_key_gain_full = lax.all_gather(barrier_set[11], ("seq", "sub"), axis=0, tiled=True)
    attn_out_gain_full = lax.all_gather(barrier_set[12], ("seq", "sub"), axis=0, tiled=True)
    barrier_set = lax.optimization_barrier(
        (gate_weight, up_weight, down_weight, ffn_gain, ffn_out_gain, video)
    )
    gate_full = lax.all_gather(barrier_set[0], ("seq", "sub"), axis=0, tiled=True)
    up_full = lax.all_gather(barrier_set[1], ("seq", "sub"), axis=0, tiled=True)
    down_full = lax.all_gather(barrier_set[2], ("seq", "sub"), axis=0, tiled=True)
    ffn_gain_full = lax.all_gather(barrier_set[3], ("seq", "sub"), axis=0, tiled=True)
    ffn_out_gain_full = lax.all_gather(barrier_set[4], ("seq", "sub"), axis=0, tiled=True)
    cond_float = conditioning.astype(jnp.float32)
    cond_act = jax.nn.silu(cond_float).astype(jnp.bfloat16)
    modulation = jnp.dot(
        cond_act, ada_full, preferred_element_type=jnp.float32
    ) + ada_bias_full.astype(jnp.float32)
    token_index = device_index * tok_rows + jnp.arange(tok_rows, dtype=jnp.int32)
    token_clip = clip_index(token_index, clip_lengths)
    clip_onehot = (token_clip[:, None] == clip_range[None, :]).astype(jnp.float32)
    per_token = jnp.dot(clip_onehot, modulation, precision=highest)
    attn_scale = per_token[:, :model_width]
    attn_gate = per_token[:, model_width : 2 * model_width]
    ffn_scale = per_token[:, 2 * model_width : 3 * model_width]
    ffn_gate = per_token[:, 3 * model_width :]
    video_float = video.astype(jnp.float32)
    video_inv = inv_rms(video_float)
    video_hat = video_float * video_inv
    attn_gain_f = attn_gain_full.astype(jnp.float32)
    attn_mult = attn_gain_f * (1.0 + attn_scale)
    normed = (video_hat * attn_mult).astype(jnp.bfloat16)
    query_pre = jnp.dot(normed, query_full, preferred_element_type=jnp.float32)
    key_pre = jnp.dot(normed, key_full, preferred_element_type=jnp.float32)
    values_tok = jnp.dot(normed, value_full, preferred_element_type=jnp.float32).astype(
        jnp.bfloat16
    )
    query_inv = inv_rms(query_pre)
    query_hat = query_pre * query_inv
    key_inv = inv_rms(key_pre)
    key_hat = key_pre * key_inv
    query_gain_f = query_gain_full.astype(jnp.float32)
    key_gain_f = key_gain_full.astype(jnp.float32)
    cosine, sine = rope_tables(positions, head_dim)
    query_tok = rotate(
        (query_hat * query_gain_f).reshape(tok_rows, heads_total, head_dim), cosine, sine
    ).astype(jnp.bfloat16)
    key_tok = rotate(
        (key_hat * key_gain_f).reshape(tok_rows, heads_total, head_dim), cosine, sine
    ).astype(jnp.bfloat16)
    query_heads, key_heads, value_heads = (
        lax.all_to_all(
            query_tok.reshape(tok_rows, model_width), "sub", split_axis=1, concat_axis=0, tiled=True
        ),
        lax.all_to_all(
            key_tok.reshape(tok_rows, model_width), "sub", split_axis=1, concat_axis=0, tiled=True
        ),
        lax.all_to_all(values_tok, "sub", split_axis=1, concat_axis=0, tiled=True),
    )
    key_all, value_all = (
        lax.all_gather(key_heads, "seq", axis=0, tiled=True),
        lax.all_gather(value_heads, "seq", axis=0, tiled=True),
    )
    group_clip = clip_index(
        seq_index * group_rows + jnp.arange(group_rows, dtype=jnp.int32), clip_lengths
    )
    query_blocks = query_heads.reshape(group_rows, heads_local, head_dim)
    key_block = min(1024, total_tokens)
    block_count = total_tokens // key_block
    key_stack = key_all.reshape(block_count, key_block, heads_local, head_dim)
    value_stack = value_all.reshape(block_count, key_block, heads_local, head_dim)
    block_starts = jnp.arange(block_count, dtype=jnp.int32) * key_block

    def block_scores(key_blk, block_start):
        key_clip = clip_index(block_start + jnp.arange(key_block, dtype=jnp.int32), clip_lengths)
        allowed = (group_clip[:, None] == key_clip[None, :])[:, None, :]
        scores = (
            jnp.einsum("qhd,khd->qhk", query_blocks, key_blk, preferred_element_type=jnp.float32)
            * score_scale
        )
        return (jnp.where(allowed, scores, masked_score), allowed)

    def forward_step(running, block_in):
        run_max, run_sum, run_acc = running
        key_blk, value_blk, block_start = block_in
        scores, allowed = block_scores(key_blk, block_start)
        new_max = jnp.maximum(run_max, jnp.max(scores, -1))
        prob_values = jnp.where(allowed, jnp.exp(scores - new_max[..., None]), 0.0)
        factor = jnp.exp(run_max - new_max)
        new_sum = run_sum * factor + jnp.sum(prob_values, -1)
        new_acc = run_acc * factor[..., None] + jnp.einsum(
            "qhk,khd->qhd",
            prob_values.astype(jnp.bfloat16),
            value_blk,
            preferred_element_type=jnp.float32,
        )
        return ((new_max, new_sum, new_acc), None)

    start_state = (
        jnp.full((group_rows, heads_local), masked_score, jnp.float32),
        jnp.zeros((group_rows, heads_local), jnp.float32),
        jnp.zeros((group_rows, heads_local, head_dim), jnp.float32),
    )
    (run_max, run_sum, run_acc), unused_out = lax.scan(
        forward_step, start_state, (key_stack, value_stack, block_starts)
    )
    self_out = run_acc / run_sum[..., None]
    log_sum = run_max + jnp.log(run_sum)
    self_tok = lax.all_to_all(
        self_out.astype(jnp.bfloat16).reshape(group_rows, heads_local * head_dim),
        "sub",
        split_axis=0,
        concat_axis=1,
        tiled=True,
    )
    cap_shard = captions.shape[0]
    cap_rows = cap_shard // num_seq
    cap_local = lax.dynamic_slice_in_dim(captions, seq_index * cap_rows, cap_rows, 0)
    text_key_pre = jnp.dot(cap_local, text_key_full, preferred_element_type=jnp.float32)
    text_inv = inv_rms(text_key_pre)
    text_hat = text_key_pre * text_inv
    text_key_gain_f = text_key_gain_full.astype(jnp.float32)
    text_keys = (text_hat * text_key_gain_f).astype(jnp.bfloat16)
    text_values = jnp.dot(cap_local, text_value_full, preferred_element_type=jnp.float32).astype(
        jnp.bfloat16
    )
    text_keys_all, text_values_all = (
        lax.all_gather(text_keys, ("seq", "sub"), axis=0, tiled=True),
        lax.all_gather(text_values, ("seq", "sub"), axis=0, tiled=True),
    )
    cap_total = text_keys_all.shape[0]
    slot_index = jnp.arange(cap_total, dtype=jnp.int32)
    owner_block = slot_index // cap_rows
    caption_row = (
        owner_block % num_sub * cap_shard
        + owner_block // num_sub * cap_rows
        + slot_index % cap_rows
    )
    caption_clip = caption_row // CAP
    clip_cap = jnp.sum(
        jnp.where(caption_clip[:, None] == clip_range[None, :], cap_lengths[None, :], 0), 1
    )
    caption_valid = caption_row % CAP < clip_cap
    text_key_heads = text_keys_all.reshape(cap_total, heads_total, head_dim)
    text_value_heads = text_values_all.reshape(cap_total, heads_total, head_dim)
    cross_allowed = ((token_clip[:, None] == caption_clip[None, :]) & caption_valid[None, :])[
        :, None, :
    ]
    cross_scores = (
        jnp.einsum("qhd,khd->qhk", query_tok, text_key_heads, preferred_element_type=jnp.float32)
        * score_scale
    )
    cross_probs = jax.nn.softmax(jnp.where(cross_allowed, cross_scores, masked_score), -1)
    cross_probs_low = cross_probs.astype(jnp.bfloat16)
    cross_out = jnp.einsum(
        "qhk,khd->qhd", cross_probs_low, text_value_heads, preferred_element_type=jnp.float32
    )
    gate_tanh = jnp.tanh(cross_gate.astype(jnp.float32))
    mixed = (
        (
            self_tok.astype(jnp.float32).reshape(tok_rows, heads_total, head_dim)
            + gate_tanh[None, :, None] * cross_out
        )
        .reshape(tok_rows, model_width)
        .astype(jnp.bfloat16)
    )
    projected = jnp.dot(mixed, out_full, preferred_element_type=jnp.float32)
    proj_inv = inv_rms(projected)
    proj_hat = projected * proj_inv
    attn_tanh = jnp.tanh(attn_gate)
    attn_out_f = attn_out_gain_full.astype(jnp.float32)
    hidden_state = video_float + attn_tanh * proj_hat * attn_out_f
    hidden_inv = inv_rms(hidden_state)
    hidden_hat = hidden_state * hidden_inv
    ffn_gain_f = ffn_gain_full.astype(jnp.float32)
    ffn_mult = ffn_gain_f * (1.0 + ffn_scale)
    ffn_in = (hidden_hat * ffn_mult).astype(jnp.bfloat16)
    gate_pre = jnp.dot(ffn_in, gate_full, preferred_element_type=jnp.float32)
    up_pre = jnp.dot(ffn_in, up_full, preferred_element_type=jnp.float32)
    activated = (jax.nn.silu(gate_pre) * up_pre).astype(jnp.bfloat16)
    down_out = jnp.dot(activated, down_full, preferred_element_type=jnp.float32)
    down_inv = inv_rms(down_out)
    down_hat = down_out * down_inv
    ffn_tanh = jnp.tanh(ffn_gate)
    ffn_out_f = ffn_out_gain_full.astype(jnp.float32)
    block_out = (hidden_state + ffn_tanh * down_hat * ffn_out_f).astype(jnp.bfloat16)
    grad_out = cotangent.astype(jnp.float32)
    ffn_gate_grad = grad_out * down_hat * ffn_out_f * (1.0 - ffn_tanh * ffn_tanh)
    ffn_out_gain_part = jnp.sum(grad_out * ffn_tanh * down_hat, 0)
    down_grad = norm_back(down_hat, down_inv, grad_out * ffn_tanh * ffn_out_f).astype(jnp.bfloat16)
    down_weight_term = jnp.einsum(
        "tf,td->fd", activated, down_grad, preferred_element_type=jnp.float32
    )
    act_grad = jnp.einsum("td,fd->tf", down_grad, down_full, preferred_element_type=jnp.float32)
    gate_sig = jax.nn.sigmoid(gate_pre)
    gate_grad = (act_grad * up_pre * gate_sig * (1.0 + gate_pre * (1.0 - gate_sig))).astype(
        jnp.bfloat16
    )
    up_grad = (act_grad * jax.nn.silu(gate_pre)).astype(jnp.bfloat16)
    gate_weight_term = jnp.einsum(
        "td,tf->df", ffn_in, gate_grad, preferred_element_type=jnp.float32
    )
    up_weight_term = jnp.einsum("td,tf->df", ffn_in, up_grad, preferred_element_type=jnp.float32)
    ffn_in_grad = jnp.einsum(
        "tf,df->td", gate_grad, gate_full, preferred_element_type=jnp.float32
    ) + jnp.einsum("tf,df->td", up_grad, up_full, preferred_element_type=jnp.float32)
    ffn_gain_part = jnp.sum(ffn_in_grad * hidden_hat * (1.0 + ffn_scale), 0)
    ffn_scale_grad = ffn_in_grad * hidden_hat * ffn_gain_f
    hidden_grad = grad_out + norm_back(hidden_hat, hidden_inv, ffn_in_grad * ffn_mult)
    attn_gate_grad = hidden_grad * proj_hat * attn_out_f * (1.0 - attn_tanh * attn_tanh)
    attn_out_gain_part = jnp.sum(hidden_grad * attn_tanh * proj_hat, 0)
    proj_grad = norm_back(proj_hat, proj_inv, hidden_grad * attn_tanh * attn_out_f).astype(
        jnp.bfloat16
    )
    out_weight_term = jnp.einsum("td,te->de", mixed, proj_grad, preferred_element_type=jnp.float32)
    mixed_grad = jnp.einsum(
        "te,de->td", proj_grad, out_full, preferred_element_type=jnp.float32
    ).astype(jnp.bfloat16)
    mixed_heads_grad = mixed_grad.astype(jnp.float32).reshape(tok_rows, heads_total, head_dim)
    cross_gate_part = jnp.sum(mixed_heads_grad * cross_out, (0, 2)) * (1.0 - gate_tanh * gate_tanh)
    cross_out_grad = (mixed_heads_grad * gate_tanh[None, :, None]).astype(jnp.bfloat16)
    cross_prob_grad = jnp.einsum(
        "qhd,khd->qhk", cross_out_grad, text_value_heads, preferred_element_type=jnp.float32
    )
    text_value_term = jnp.einsum(
        "qhk,qhd->khd", cross_probs_low, cross_out_grad, preferred_element_type=jnp.float32
    )
    cross_delta = jnp.sum(cross_probs * cross_prob_grad, -1, keepdims=True)
    cross_score_grad = (cross_probs * (cross_prob_grad - cross_delta)).astype(jnp.bfloat16)
    query_cross_grad = (
        jnp.einsum(
            "qhk,khd->qhd", cross_score_grad, text_key_heads, preferred_element_type=jnp.float32
        )
        * score_scale
    )
    text_key_term = (
        jnp.einsum("qhk,qhd->khd", cross_score_grad, query_tok, preferred_element_type=jnp.float32)
        * score_scale
    )
    dout_flat = lax.all_to_all(mixed_grad, "sub", split_axis=1, concat_axis=0, tiled=True)
    dout_heads = dout_flat.reshape(group_rows, heads_local, head_dim)
    self_delta = jnp.sum(dout_heads.astype(jnp.float32) * self_out, -1)

    def backward_step(query_acc, block_in):
        key_blk, value_blk, block_start = block_in
        scores, allowed = block_scores(key_blk, block_start)
        prob_values = jnp.where(allowed, jnp.exp(scores - log_sum[..., None]), 0.0)
        prob_grad = jnp.einsum(
            "qhd,khd->qhk", dout_heads, value_blk, preferred_element_type=jnp.float32
        )
        value_term = jnp.einsum(
            "qhk,qhd->khd",
            prob_values.astype(jnp.bfloat16),
            dout_heads,
            preferred_element_type=jnp.float32,
        )
        score_grad = (prob_values * (prob_grad - self_delta[..., None])).astype(jnp.bfloat16)
        query_acc = (
            query_acc
            + jnp.einsum("qhk,khd->qhd", score_grad, key_blk, preferred_element_type=jnp.float32)
            * score_scale
        )
        key_term = (
            jnp.einsum("qhk,qhd->khd", score_grad, query_blocks, preferred_element_type=jnp.float32)
            * score_scale
        )
        return (query_acc, (key_term, value_term))

    query_zero = jnp.zeros((group_rows, heads_local, head_dim), jnp.float32)
    query_self_grad, (key_terms, value_terms) = lax.scan(
        backward_step, query_zero, (key_stack, value_stack, block_starts)
    )
    key_grad_heads, value_grad_heads = (
        lax.psum_scatter(
            key_terms.reshape(total_tokens, heads_local * head_dim).astype(jnp.bfloat16),
            "seq",
            scatter_dimension=0,
            tiled=True,
        ).astype(jnp.float32),
        lax.psum_scatter(
            value_terms.reshape(total_tokens, heads_local * head_dim).astype(jnp.bfloat16),
            "seq",
            scatter_dimension=0,
            tiled=True,
        ).astype(jnp.float32),
    )
    query_back, key_back, value_back = (
        lax.all_to_all(
            query_self_grad.reshape(group_rows, heads_local * head_dim).astype(jnp.bfloat16),
            "sub",
            split_axis=0,
            concat_axis=1,
            tiled=True,
        ).astype(jnp.float32),
        lax.all_to_all(
            round_keep(key_grad_heads).astype(jnp.bfloat16),
            "sub",
            split_axis=0,
            concat_axis=1,
            tiled=True,
        ).astype(jnp.float32),
        lax.all_to_all(
            round_keep(value_grad_heads).astype(jnp.bfloat16),
            "sub",
            split_axis=0,
            concat_axis=1,
            tiled=True,
        ).astype(jnp.float32),
    )
    query_rot_grad = round_keep(
        query_back.reshape(tok_rows, heads_total, head_dim) + query_cross_grad
    )
    query_norm_grad = rotate(query_rot_grad, cosine, -sine).reshape(tok_rows, model_width)
    query_gain_part = jnp.sum(query_norm_grad * query_hat, 0)
    query_pre_grad = norm_back(query_hat, query_inv, query_norm_grad * query_gain_f).astype(
        jnp.bfloat16
    )
    key_norm_grad = rotate(
        key_back.reshape(tok_rows, heads_total, head_dim), cosine, -sine
    ).reshape(tok_rows, model_width)
    key_gain_part = jnp.sum(key_norm_grad * key_hat, 0)
    key_pre_grad = norm_back(key_hat, key_inv, key_norm_grad * key_gain_f).astype(jnp.bfloat16)
    value_grad = value_back.astype(jnp.bfloat16)
    query_weight_term = jnp.einsum(
        "td,te->de", normed, query_pre_grad, preferred_element_type=jnp.float32
    )
    key_weight_term = jnp.einsum(
        "td,te->de", normed, key_pre_grad, preferred_element_type=jnp.float32
    )
    value_weight_term = jnp.einsum(
        "td,te->de", normed, value_grad, preferred_element_type=jnp.float32
    )
    normed_grad = (
        jnp.einsum("te,de->td", query_pre_grad, query_full, preferred_element_type=jnp.float32)
        + jnp.einsum("te,de->td", key_pre_grad, key_full, preferred_element_type=jnp.float32)
        + jnp.einsum("te,de->td", value_grad, value_full, preferred_element_type=jnp.float32)
    )
    attn_gain_part = jnp.sum(normed_grad * video_hat * (1.0 + attn_scale), 0)
    attn_scale_grad = normed_grad * video_hat * attn_gain_f
    video_grad = hidden_grad + norm_back(video_hat, video_inv, normed_grad * attn_mult)
    text_key_sum, text_value_sum = (
        lax.psum_scatter(
            text_key_term.reshape(cap_total, model_width),
            ("seq", "sub"),
            scatter_dimension=0,
            tiled=True,
        ),
        lax.psum_scatter(
            text_value_term.reshape(cap_total, model_width),
            ("seq", "sub"),
            scatter_dimension=0,
            tiled=True,
        ),
    )
    text_key_low = round_keep(text_key_sum)
    text_value_low = text_value_sum.astype(jnp.bfloat16)
    text_key_gain_part = jnp.sum(text_key_low * text_hat, 0)
    text_key_pre_grad = norm_back(text_hat, text_inv, text_key_low * text_key_gain_f).astype(
        jnp.bfloat16
    )
    text_key_weight_term = jnp.einsum(
        "tc,td->cd", cap_local, text_key_pre_grad, preferred_element_type=jnp.float32
    )
    text_value_weight_term = jnp.einsum(
        "tc,td->cd", cap_local, text_value_low, preferred_element_type=jnp.float32
    )
    caption_rows_grad = jnp.einsum(
        "td,cd->tc", text_key_pre_grad, text_key_full, preferred_element_type=jnp.float32
    ) + jnp.einsum("td,cd->tc", text_value_low, text_value_full, preferred_element_type=jnp.float32)
    caption_grad = lax.all_gather(
        caption_rows_grad.astype(jnp.bfloat16), "seq", axis=0, tiled=True
    ).astype(caption_rows_grad.dtype)
    token_mod_grad = jnp.concatenate(
        [attn_scale_grad, attn_gate_grad, ffn_scale_grad, ffn_gate_grad], 1
    )
    mod_part = jnp.einsum("tc,tm->cm", clip_onehot, token_mod_grad, precision=highest)
    mod_sum, gate_sum = lax.psum((mod_part, cross_gate_part), ("seq", "sub"))
    mod_low = mod_sum.astype(jnp.bfloat16)
    bias_rows = ada_bias.shape[0]
    ada_bias_grad = jnp.sum(
        lax.dynamic_slice_in_dim(
            mod_low.astype(jnp.float32), device_index * bias_rows, bias_rows, 1
        ),
        0,
    )
    cond_rows = ada_weight.shape[0]
    cond_slice = lax.dynamic_slice_in_dim(cond_act, device_index * cond_rows, cond_rows, 1)
    ada_weight_grad = jnp.einsum(
        "cr,cm->rm", cond_slice, mod_low, preferred_element_type=jnp.float32
    )
    cond_sig = jax.nn.sigmoid(cond_float)
    cond_grad = (
        jnp.einsum("cm,rm->cr", mod_low, ada_full, preferred_element_type=jnp.float32)
        * cond_sig
        * (1.0 + cond_float * (1.0 - cond_sig))
    )
    (
        query_weight_grad,
        key_weight_grad,
        value_weight_grad,
        out_weight_grad,
        text_key_weight_grad,
        text_value_weight_grad,
        attn_gain_grad,
        query_gain_grad,
        key_gain_grad,
        text_key_gain_grad,
        attn_out_gain_grad,
    ) = (
        lax.psum_scatter(query_weight_term, ("seq", "sub"), scatter_dimension=0, tiled=True),
        lax.psum_scatter(key_weight_term, ("seq", "sub"), scatter_dimension=0, tiled=True),
        lax.psum_scatter(value_weight_term, ("seq", "sub"), scatter_dimension=0, tiled=True),
        lax.psum_scatter(out_weight_term, ("seq", "sub"), scatter_dimension=0, tiled=True),
        lax.psum_scatter(text_key_weight_term, ("seq", "sub"), scatter_dimension=0, tiled=True),
        lax.psum_scatter(text_value_weight_term, ("seq", "sub"), scatter_dimension=0, tiled=True),
        lax.psum_scatter(attn_gain_part, ("seq", "sub"), scatter_dimension=0, tiled=True),
        lax.psum_scatter(query_gain_part, ("seq", "sub"), scatter_dimension=0, tiled=True),
        lax.psum_scatter(key_gain_part, ("seq", "sub"), scatter_dimension=0, tiled=True),
        lax.psum_scatter(text_key_gain_part, ("seq", "sub"), scatter_dimension=0, tiled=True),
        lax.psum_scatter(attn_out_gain_part, ("seq", "sub"), scatter_dimension=0, tiled=True),
    )
    gate_weight_grad, up_weight_grad, down_weight_grad, ffn_gain_grad, ffn_out_gain_grad = (
        lax.psum_scatter(gate_weight_term, ("seq", "sub"), scatter_dimension=0, tiled=True),
        lax.psum_scatter(up_weight_term, ("seq", "sub"), scatter_dimension=0, tiled=True),
        lax.psum_scatter(down_weight_term, ("seq", "sub"), scatter_dimension=0, tiled=True),
        lax.psum_scatter(ffn_gain_part, ("seq", "sub"), scatter_dimension=0, tiled=True),
        lax.psum_scatter(ffn_out_gain_part, ("seq", "sub"), scatter_dimension=0, tiled=True),
    )
    return (
        block_out,
        video_grad,
        caption_grad,
        cond_grad,
        ada_weight_grad,
        ada_bias_grad,
        query_weight_grad,
        key_weight_grad,
        value_weight_grad,
        out_weight_grad,
        text_key_weight_grad,
        text_value_weight_grad,
        gate_weight_grad,
        up_weight_grad,
        down_weight_grad,
        attn_gain_grad,
        query_gain_grad,
        key_gain_grad,
        text_key_gain_grad,
        attn_out_gain_grad,
        ffn_gain_grad,
        ffn_out_gain_grad,
        gate_sum,
    )


def solution(mesh):
    placed = (
        P(("seq", "sub"), None),
        P(),
        P("sub", None),
        P(),
        P(),
        P(("seq", "sub"), None),
        P(("seq", "sub"), None),
        P(("seq", "sub")),
        P(("seq", "sub"), None),
        P(("seq", "sub"), None),
        P(("seq", "sub"), None),
        P(("seq", "sub"), None),
        P(("seq", "sub"), None),
        P(("seq", "sub"), None),
        P(("seq", "sub"), None),
        P(("seq", "sub"), None),
        P(("seq", "sub"), None),
        P(("seq", "sub")),
        P(("seq", "sub")),
        P(("seq", "sub")),
        P(("seq", "sub")),
        P(("seq", "sub")),
        P(("seq", "sub")),
        P(("seq", "sub")),
        P(),
        P(("seq", "sub"), None),
    )
    return jax.shard_map(
        body,
        mesh=mesh,
        in_specs=placed,
        out_specs=(
            P(("seq", "sub"), None),
            P(("seq", "sub"), None),
            P("sub", None),
            P(),
            P(("seq", "sub"), None),
            P(("seq", "sub")),
            P(("seq", "sub"), None),
            P(("seq", "sub"), None),
            P(("seq", "sub"), None),
            P(("seq", "sub"), None),
            P(("seq", "sub"), None),
            P(("seq", "sub"), None),
            P(("seq", "sub"), None),
            P(("seq", "sub"), None),
            P(("seq", "sub"), None),
            P(("seq", "sub")),
            P(("seq", "sub")),
            P(("seq", "sub")),
            P(("seq", "sub")),
            P(("seq", "sub")),
            P(("seq", "sub")),
            P(("seq", "sub")),
            P(),
        ),
        check_vma=False,
    )
```

profile of v0, /device:TPU:0, one launch (start us, length us, event | category | flops | bytes accessed | tf_op | source)
XLA Modules:
  0.0 3339.4 jit_solution(13927837446089272986)
XLA Ops:
  18.0 43.8 %all-reduce.16 = (bf16[6144]{0:T(1024)(128)(2,1)S(1)}, bf16[1536]{0:T(1024)(128)(2,1)S(1)}, bf16[1536]{0:T(1024)(128)(2,1)S(1)}, bf16[1536]{0:T(1024)(128)(2,1)S...) all-reduce(bf16[6144]{0:T(1024)(128)(2,1)S(1)} %dynamic-update-slic, ...), channel_id=1, replica_groups=mesh['seq'=8,'sub'=4] {'seq','sub'}, use_global_device_ids=true, to_apply=%add | all-reduce | flops 16896 | bytes 67584
  66.8 42.4 %all-gather.16.cloned.1.call-done = bf16[1024,6144]{1,0:T(8,128)(2,1)} async-done(((bf16[32,6144]{1,0:T(8,128)(2,1)}), bf16[1024,6144]{1,0:T(8,128)(2,1)}) %all-gather.16.cloned.1.call-update) | async-done | bytes 12582928 | tf_op jit(solution)/shard_map/all_gather | solution.py:119
  118.8 55.4 %all-gather.18.cloned.1.call-done = bf16[1536,1536]{1,0:T(8,128)(2,1)} async-done(((bf16[48,1536]{1,0:T(8,128)(2,1)}), bf16[1536,1536]{1,0:T(8,128)(2,1)}) %all-gather.18.cloned.1.call-update) | async-done | bytes 4718608 | tf_op jit(solution)/shard_map/all_gather | solution.py:122
  184.9 16.7 all_to_all.119
  202.6 38.3 %all-gather.24.cloned.1.call-done = bf16[1536,1536]{1,0:T(8,128)(2,1)} async-done(((bf16[48,1536]{1,0:T(8,128)(2,1)}), bf16[1536,1536]{1,0:T(8,128)(2,1)}) %all-gather.24.cloned.1.call-update) | async-done | bytes 4718608 | tf_op jit(solution)/shard_map/all_gather | solution.py:123
  244.1 22.2 all_to_all.120
  266.6 73.8 %all-gather.32.cloned.1.call-done = bf16[4096,1536]{1,0:T(8,128)(2,1)} async-done(((bf16[128,1536]{1,0:T(8,128)(2,1)}), bf16[4096,1536]{1,0:T(8,128)(2,1)}) %all-gather.32.cloned.1.call-update) | async-done | bytes 12582928 | tf_op jit(solution)/shard_map/all_gather | solution.py:125
  348.7 88.2 %all-gather.28.cloned.1.call-done = bf16[4096,1536]{1,0:T(8,128)(2,1)} async-done(((bf16[128,1536]{1,0:T(8,128)(2,1)}), bf16[4096,1536]{1,0:T(8,128)(2,1)}) %all-gather.28.cloned.1.call-update) | async-done | bytes 12582928 | tf_op jit(solution)/shard_map/all_gather | solution.py:126
  447.0 54.8 %all-gather.22.cloned.1.call-done = bf16[1536,1536]{1,0:T(8,128)(2,1)} async-done(((bf16[48,1536]{1,0:T(8,128)(2,1)}), bf16[1536,1536]{1,0:T(8,128)(2,1)}) %all-gather.22.cloned.1.call-update) | async-done | bytes 4718608 | tf_op jit(solution)/shard_map/all_gather | solution.py:121
  550.3 18.6 all-gather.26.cloned.1.call-done
  584.3 106.8 %while.34 = (s32[]{:T(128)}, f32[512,6]{0,1:T(8,128)S(1)}, f32[512,6]{0,1:T(8,128)}, f32[512,6,64]{0,2,1:T(8,128)}, s32[512]{0:T(512)}, /*index=5*/s32[4]{0:T(12...) while((s32[]{:T(128)}, f32[512,6]{0,1:T(8,128)S(1)}, ...), condition=%wide.region_10.11_spmd.clone, body=%wide.region_6.10_spmd.clone.sunk | while | flops 847345664 | bytes 94031096 | solution.py:230
  702.6 10.2 all-to-all-done.3
  726.4 19.0 fusion.152
  745.4 9.3 add_convert_fusion.1
  767.7 90.5 %all-gather.38.cloned.1.call-done = bf16[1536,4096]{1,0:T(8,128)(2,1)} async-done(((bf16[48,4096]{1,0:T(8,128)(2,1)}), bf16[1536,4096]{1,0:T(8,128)(2,1)}) %all-gather.38.cloned.1.call-update) | async-done | bytes 12582928 | tf_op jit(solution)/shard_map/all_gather | solution.py:135
  865.9 89.0 %all-gather.40.cloned.1.call-done = bf16[1536,4096]{1,0:T(8,128)(2,1)} async-done(((bf16[48,4096]{1,0:T(8,128)(2,1)}), bf16[1536,4096]{1,0:T(8,128)(2,1)}) %all-gather.40.cloned.1.call-update) | async-done | bytes 12582928 | tf_op jit(solution)/shard_map/all_gather | solution.py:136
  954.9 9.0 multiply_convert_fusion.2
  963.9 87.6 %all-gather.42.cloned.1.call-done = bf16[4096,1536]{1,0:T(8,128)(2,1)} async-done(((bf16[128,1536]{1,0:T(8,128)(2,1)}), bf16[4096,1536]{1,0:T(8,128)(2,1)}) %all-gather.42.cloned.1.call-update) | async-done | bytes 12582928 | tf_op jit(solution)/shard_map/all_gather | solution.py:137
  1061.0 10.2 multiply_convert_fusion
  1071.1 10.0 fusion.154
  1081.2 9.8 multiply_reduce_fusion.2
  1097.2 12.2 fusion.50
  1109.4 10.8 fusion.52
  1127.5 9.2 copy.244
  1142.3 12.5 fusion.58
  1154.8 9.3 copy.256
  1169.1 131.6 %while.35 = (s32[]{:T(128)}, f32[512,6,64]{0,2,1:T(8,128)}, bf16[4,1024,6,64]{1,3,2,0:T(8,128)(2,1)}, bf16[4,1024,6,64]{1,3,2,0:T(8,128)(2,1)}, bf16[4,1024,6,64...) while((s32[]{:T(128)}, f32[512,6,64]{0,2,1:T(8,128)}, ...), condition=%wide.region_24.25_spmd.clone, body=%wide.region_22.24_spmd.clone.sunk | while | flops 2052537344 | bytes 142549840 | solution.py:396
  1225.6 9.0 bitcast_dynamic-update-slice_fusion.5
  1290.9 9.5 bitcast_dynamic-update-slice_fusion.5
  1316.9 69.3 %reduce-scatter.40.cloned.1.call-done = f32[40,1536]{1,0:T(8,128)} async-done(((f32[1280,1536]{1,0:T(8,128)}), f32[40,1536]{1,0:T(8,128)}) %reduce-scatter.40.cloned.1.call-update) | async-done | bytes 245776
  1396.2 10.2 fusion.57
  1415.5 13.1 all_to_all.121
  1487.5 13.9 all_to_all.122
  1507.4 11.6 fusion.163
  1520.0 11.7 fusion.161
  1531.8 12.3 fusion.162
  1545.2 11.1 fusion.101
  1556.3 10.7 fusion.103
  1585.3 43.3 %all-reduce.18 = (bf16[5,6144]{1,0:T(8,128)(2,1)S(1)}, f32[1536]{0:T(1024)S(1)}, f32[1536]{0:T(1024)S(1)}, f32[1536]{0:T(1024)S(1)}, f32[1536]{0:T(1024)S(1)}, /...) all-reduce(f32[5,6144]{1,0:T(8,128)S(1)} %fusion.62, ...), channel_id=1, replica_groups=mesh['seq'=8,'sub'=4] {'seq','sub'}, use_global_device_ids=true, to_apply=%region_34.35 | all-reduce | flops 41496 | bytes 270528 | tf_op jit(solution)/shard_map/psum | solution.py:503
  1648.1 11.9 reduce-scatter.28.cloned.1.call-done
  1660.0 141.7 %reduce-scatter.24.cloned.1.call-done = f32[48,1536]{1,0:T(8,128)} async-done(((f32[1536,1536]{1,0:T(8,128)}), f32[48,1536]{1,0:T(8,128)}) %reduce-scatter.24.cloned.1.call-update) | async-done | bytes 294928 | tf_op jit(solution)/shard_map/reduce_scatter | solution.py:537
  1801.6 141.7 %reduce-scatter.22.cloned.1.call-done = f32[48,1536]{1,0:T(8,128)} async-done(((f32[1536,1536]{1,0:T(8,128)}), f32[48,1536]{1,0:T(8,128)}) %reduce-scatter.22.cloned.1.call-update) | async-done | bytes 294928 | tf_op jit(solution)/shard_map/reduce_scatter | solution.py:536
  1943.3 141.7 %reduce-scatter.26.cloned.1.call-done = f32[48,1536]{1,0:T(8,128)} async-done(((f32[1536,1536]{1,0:T(8,128)}), f32[48,1536]{1,0:T(8,128)}) %reduce-scatter.26.cloned.1.call-update) | async-done | bytes 294928 | tf_op jit(solution)/shard_map/reduce_scatter | solution.py:538
  2085.0 248.9 %reduce-scatter.38.cloned.1.call-done = f32[128,1536]{1,0:T(8,128)} async-done(((f32[4096,1536]{1,0:T(8,128)}), f32[128,1536]{1,0:T(8,128)}) %reduce-scatter.38.cloned.1.call-update) | async-done | bytes 786448 | tf_op jit(solution)/shard_map/reduce_scatter | solution.py:551
  2333.9 249.6 %reduce-scatter.34.cloned.1.call-done = f32[48,4096]{1,0:T(8,128)} async-done(((f32[1536,4096]{1,0:T(8,128)}), f32[48,4096]{1,0:T(8,128)}) %reduce-scatter.34.cloned.1.call-update) | async-done | bytes 786448 | tf_op jit(solution)/shard_map/reduce_scatter | solution.py:549
  2583.5 249.5 %reduce-scatter.36.cloned.1.call-done = f32[48,4096]{1,0:T(8,128)} async-done(((f32[1536,4096]{1,0:T(8,128)}), f32[48,4096]{1,0:T(8,128)}) %reduce-scatter.36.cloned.1.call-update) | async-done | bytes 786448 | tf_op jit(solution)/shard_map/reduce_scatter | solution.py:550
  2833.0 249.5 %reduce-scatter.32.cloned.1.call-done = f32[128,1536]{1,0:T(8,128)} async-done(((f32[4096,1536]{1,0:T(8,128)}), f32[128,1536]{1,0:T(8,128)}) %reduce-scatter.32.cloned.1.call-update) | async-done | bytes 786448 | tf_op jit(solution)/shard_map/reduce_scatter | solution.py:541
  3082.5 249.6 %reduce-scatter.30.cloned.1.call-done = f32[128,1536]{1,0:T(8,128)} async-done(((f32[4096,1536]{1,0:T(8,128)}), f32[128,1536]{1,0:T(8,128)}) %reduce-scatter.30.cloned.1.call-update) | async-done | bytes 786448 | tf_op jit(solution)/shard_map/reduce_scatter | solution.py:540
  (525 shorter events, 560.2 us)
Async XLA Ops:
  7.2 333.2 %copy-start = (bf16[320,4096]{1,0:T(8,128)(2,1)S(1)}, bf16[320,4096]{1,0:T(8,128)(2,1)}, u32[]{:S(2)}) copy-start(bf16[320,4096]{1,0:T(8,128)(2,1)} %param.32) | copy-start | bytes 7864324
  7.2 102.0 %all-gather.16.cloned.1.call-start = ((), (), s32[]{:S(2)}) async-start(), calls=%async_computation.21 | async-start | bytes 12976128 | tf_op jit(solution)/shard_map/all_gather | solution.py:119
  7.9 166.3 %all-gather.18.cloned.1.call-start = ((), (), s32[]{:S(2)}) async-start(), calls=%async_computation.22 | async-start | bytes 4866048 | tf_op jit(solution)/shard_map/all_gather | solution.py:122
  8.7 232.2 %all-gather.24.cloned.1.call-start = ((), (), s32[]{:S(2)}) async-start(), calls=%async_computation.25 | async-start | bytes 4866048 | tf_op jit(solution)/shard_map/all_gather | solution.py:123
  9.4 331.0 %all-gather.32.cloned.1.call-start = ((), (), s32[]{:S(2)}) async-start(), calls=%async_computation.29 | async-start | bytes 12976128 | tf_op jit(solution)/shard_map/all_gather | solution.py:125
  10.0 427.0 %all-gather.28.cloned.1.call-start = ((), (), s32[]{:S(2)}) async-start(), calls=%async_computation.27 | async-start | bytes 12976128 | tf_op jit(solution)/shard_map/all_gather | solution.py:126
  10.6 491.2 %all-gather.22.cloned.1.call-start = ((), (), s32[]{:S(2)}) async-start(), calls=%async_computation.24 | async-start | bytes 4866048 | tf_op jit(solution)/shard_map/all_gather | solution.py:121
  11.2 523.6 %all-gather.20.cloned.1.call-start = ((), (), s32[]{:S(2)}) async-start(), calls=%async_computation.23 | async-start | bytes 3538944 | tf_op jit(solution)/shard_map/all_gather | solution.py:187
  61.8 55.2 %copy-start.52 = (f32[1536]{0:T(1024)}, f32[1536]{0:T(1024)S(1)}, u32[]{:S(2)}) copy-start(f32[1536]{0:T(1024)S(1)} %convert_element_type.257) | copy-start | bytes 18436
  61.9 115.6 %copy-start.54 = (f32[1536]{0:T(1024)}, f32[1536]{0:T(1024)S(1)}, u32[]{:S(2)}) copy-start(f32[1536]{0:T(1024)S(1)} %convert_element_type.259) | copy-start | bytes 18436
  64.9 443.4 %copy-start.45 = (f32[128,32]{0,1:T(8,128)}, f32[128,32]{0,1:T(8,128)S(1)}, u32[]{:S(2)}) copy-start(f32[128,32]{0,1:T(8,128)S(1)} %get-tuple-element.628) | copy-start | bytes 49156
  66.8 50.2 %copy-start.68 = (f32[128]{0:T(128)}, f32[128]{0:T(128)S(1)}, u32[]{:S(2)}) copy-start(f32[128]{0:T(128)S(1)} %add_rsqrt_fusion.6) | copy-start | bytes 1540
  66.8 51.9 %copy-start.20 = (bf16[128,1536]{1,0:T(8,128)(2,1)S(1)}, bf16[128,1536]{1,0:T(8,128)(2,1)}, u32[]{:S(2)}) copy-start(bf16[128,1536]{1,0:T(8,128)(2,1)} %param.30) | copy-start | bytes 1179652
  118.8 383.0 %copy-start.10 = (bf16[128,1536]{1,0:T(8,128)(2,1)}, bf16[128,1536]{1,0:T(8,128)(2,1)S(1)}, u32[]{:S(2)}) copy-start(bf16[128,1536]{1,0:T(8,128)(2,1)S(1)} %fusion.84) | copy-start | bytes 1179652
  177.4 66.6 %copy-start.70 = (f32[128]{0:T(128)}, f32[128]{0:T(128)S(1)}, u32[]{:S(2)}) copy-start(f32[128]{0:T(128)S(1)} %add_rsqrt_fusion.5) | copy-start | bytes 1540
  202.6 366.3 %all-gather.26.cloned.1.call-start = ((), (), s32[]{:S(2)}) async-start(), calls=%async_computation.26 | async-start | bytes 3538944 | tf_op jit(solution)/shard_map/all_gather | solution.py:188
  266.3 447.4 %all-gather.34.cloned.1.call-start = ((), (), s32[]{:S(2)}) async-start(), calls=%async_computation.30 | async-start | bytes 4055040 | tf_op jit(solution)/shard_map/all_gather | solution.py:254
  266.6 80.6 %copy-start.58 = (f32[1536]{0:T(1024)}, f32[1536]{0:T(1024)S(1)}, u32[]{:S(2)}) copy-start(f32[1536]{0:T(1024)S(1)} %convert_element_type.274) | copy-start | bytes 18436
  347.2 97.1 %copy-start.74 = (f32[40]{0:T(128)}, f32[40]{0:T(128)S(1)}, u32[]{:S(2)}) copy-start(f32[40]{0:T(128)S(1)} %add_rsqrt_fusion.3) | copy-start | bytes 484
  348.7 371.4 %all-gather.30.cloned.1.call-start = ((), (), s32[]{:S(2)}) async-start(), calls=%async_computation.28 | async-start | bytes 4055040 | tf_op jit(solution)/shard_map/all_gather | solution.py:255
  444.4 317.5 %all-gather.36.cloned.1.call-start = ((), (), s32[]{:S(2)}) async-start(), calls=%async_computation.31 | async-start | bytes 4866048 | tf_op jit(solution)/shard_map/all_gather | solution.py:124
  445.1 413.1 %all-gather.38.cloned.1.call-start = ((), (), s32[]{:S(2)}) async-start(), calls=%async_computation.32 | async-start | bytes 12976128 | tf_op jit(solution)/shard_map/all_gather | solution.py:135
  445.7 509.3 %all-gather.40.cloned.1.call-start = ((), (), s32[]{:S(2)}) async-start(), calls=%async_computation.33 | async-start | bytes 12976128 | tf_op jit(solution)/shard_map/all_gather | solution.py:136
  446.4 605.1 %all-gather.42.cloned.1.call-start = ((), (), s32[]{:S(2)}) async-start(), calls=%async_computation.34 | async-start | bytes 12976128 | tf_op jit(solution)/shard_map/all_gather | solution.py:137
  447.0 58.0 %copy-start.56 = (f32[1536]{0:T(1024)}, f32[1536]{0:T(1024)S(1)}, u32[]{:S(2)}) copy-start(f32[1536]{0:T(1024)S(1)} %convert_element_type.264) | copy-start | bytes 18436
  447.0 71.1 %copy-start.78 = (s32[5]{0:T(128)S(1)}, s32[5]{0:T(128)}, u32[]{:S(2)}) copy-start(s32[5]{0:T(128)} %param.34) | copy-start | bytes 64
  511.0 15.8 all-to-all-start.1
  695.0 17.8 all-to-all-start.3
  699.7 616.2 %reduce-scatter.20.cloned.1.call-start = ((), (), s32[]{:S(2)}) async-start(), calls=%async_computation.37 | async-start | bytes 8110080 | tf_op jit(solution)/shard_map/reduce_scatter | solution.py:468
  767.7 187.2 %copy-start.23 = (bf16[128,1536]{1,0:T(8,128)(2,1)}, bf16[128,1536]{1,0:T(8,128)(2,1)S(1)}, u32[]{:S(2)}) copy-start(bf16[128,1536]{1,0:T(8,128)(2,1)S(1)} %multiply_convert_fusion.8) | copy-start | bytes 1179652
  1138.8 25.4 all-to-all-start.4
  1142.3 244.0 %reduce-scatter.40.cloned.1.call-start = ((), (), s32[]{:S(2)}) async-start(), calls=%async_computation.48 | async-start | bytes 8110080
  1164.2 271.0 %reduce-scatter.16.cloned.1.call-start = ((), (), s32[]{:S(2)}) async-start(), calls=%async_computation.35 | async-start | bytes 3538944 | tf_op jit(solution)/shard_map/reduce_scatter | solution.py:400
  1308.3 178.1 %reduce-scatter.18.cloned.1.call-start = ((), (), s32[]{:S(2)}) async-start(), calls=%async_computation.36 | async-start | bytes 3538944 | tf_op jit(solution)/shard_map/reduce_scatter | solution.py:406
  1312.7 74.8 %copy-start.28 = (f32[40,1536]{1,0:T(8,128)S(1)}, f32[40,1536]{1,0:T(8,128)}, u32[]{:S(2)}) copy-start(f32[40,1536]{1,0:T(8,128)} %copy-done.27) | copy-start | bytes 737284
  1312.7 74.8 %copy-start.59 = (f32[1536]{0:T(1024)S(1)}, f32[1536]{0:T(1024)}, u32[]{:S(2)}) copy-start(f32[1536]{0:T(1024)} %copy-done.58) | copy-start | bytes 18436
  1312.7 74.8 %copy-start.75 = (f32[40]{0:T(128)S(1)}, f32[40]{0:T(128)}, u32[]{:S(2)}) copy-start(f32[40]{0:T(128)} %copy-done.74) | copy-start | bytes 484
  1315.9 327.4 %all-gather.44.cloned.1.call-start = ((), (), s32[]{:S(2)}) async-start(), calls=%async_computation.38 | async-start | bytes 2949120 | tf_op jit(solution)/shard_map/all_gather | solution.py:496
  1406.4 253.6 %reduce-scatter.28.cloned.1.call-start = ((), (), s32[]{:S(2)}) async-start(), calls=%async_computation.42 | async-start | bytes 9732096 | tf_op jit(solution)/shard_map/reduce_scatter | solution.py:539
  1437.0 16.2 all-to-all-start.6
  1441.6 360.0 %reduce-scatter.24.cloned.1.call-start = ((), (), s32[]{:S(2)}) async-start(), calls=%async_computation.40 | async-start | bytes 9732096 | tf_op jit(solution)/shard_map/reduce_scatter | solution.py:537
  1475.0 468.3 %reduce-scatter.22.cloned.1.call-start = ((), (), s32[]{:S(2)}) async-start(), calls=%async_computation.39 | async-start | bytes 9732096 | tf_op jit(solution)/shard_map/reduce_scatter | solution.py:536
  1486.3 598.6 %reduce-scatter.26.cloned.1.call-start = ((), (), s32[]{:S(2)}) async-start(), calls=%async_computation.41 | async-start | bytes 9732096 | tf_op jit(solution)/shard_map/reduce_scatter | solution.py:538
  1506.4 827.5 %reduce-scatter.38.cloned.1.call-start = ((), (), s32[]{:S(2)}) async-start(), calls=%async_computation.47 | async-start | bytes 25952256 | tf_op jit(solution)/shard_map/reduce_scatter | solution.py:551
  1519.0 1064.5 %reduce-scatter.34.cloned.1.call-start = ((), (), s32[]{:S(2)}) async-start(), calls=%async_computation.45 | async-start | bytes 25952256 | tf_op jit(solution)/shard_map/reduce_scatter | solution.py:549
  1531.8 1301.2 %reduce-scatter.36.cloned.1.call-start = ((), (), s32[]{:S(2)}) async-start(), calls=%async_computation.46 | async-start | bytes 25952256 | tf_op jit(solution)/shard_map/reduce_scatter | solution.py:550
  1544.2 1538.3 %reduce-scatter.32.cloned.1.call-start = ((), (), s32[]{:S(2)}) async-start(), calls=%async_computation.44 | async-start | bytes 25952256 | tf_op jit(solution)/shard_map/reduce_scatter | solution.py:541
  1556.2 1775.9 %reduce-scatter.30.cloned.1.call-start = ((), (), s32[]{:S(2)}) async-start(), calls=%async_computation.43 | async-start | bytes 25952256 | tf_op jit(solution)/shard_map/reduce_scatter | solution.py:540
  (92 other events, 676.8 us)
Sparse Core Ops, SparseCore 0:
  10.9 98.2 all-gather.15
  112.0 62.1 all-gather.17
  177.0 63.8 all-gather.23
  243.6 96.7 all-gather.31
  343.1 93.7 all-gather.27
  439.6 62.1 all-gather.21
  504.3 30.4 all-gather.19
  536.7 32.1 all-gather.25
  572.3 60.9 all-gather.33
  636.5 59.7 all-gather.29
  699.1 62.7 all-gather.35
  764.6 93.5 all-gather.37
  861.1 93.7 all-gather.39
  957.7 93.7 all-gather.41
  1136.8 121.7 reduce-scatter.19
  1264.1 122.1 reduce-scatter.39
  1390.1 44.9 reduce-scatter.15
  1438.4 46.0 reduce-scatter.17
  1486.3 29.9 all-gather.43
  1522.6 137.2 reduce-scatter.27
  1666.4 135.1 reduce-scatter.23
  1808.1 135.1 reduce-scatter.21
  1949.8 135.1 reduce-scatter.25
  2091.8 242.0 reduce-scatter.37
  2340.9 242.5 reduce-scatter.33
  2590.4 242.5 reduce-scatter.35
  2839.8 242.5 reduce-scatter.31
  3089.5 242.5 reduce-scatter.29
where the time goes:
time: 3350 us; the launch traced here: 3340 us
  waiting for transfers between devices  2440 us (73%)
  matrix products  440 us (13%)
  local copies, waits for them, and re-layouts  155 us (5%)
  blocking collectives  153 us (5%)
  other arithmetic  117 us (3%)
    reduce_scatter x1, waiting for transfers between devices, body(): lax.psum_scatter(gate_weight_term, ('seq', 'sub'), scatter_dimension=0, t...  250 us
    reduce_scatter x1, waiting for transfers between devices, body(): lax.psum_scatter(text_key_weight_term, ('seq', 'sub'), scatter_dimension=...  250 us
    reduce_scatter x1, waiting for transfers between devices, body(): lax.psum_scatter(up_weight_term, ('seq', 'sub'), scatter_dimension=0, til...  249 us
    reduce_scatter x1, waiting for transfers between devices, body(): lax.psum_scatter(text_value_weight_term, ('seq', 'sub'), scatter_dimensio...  249 us
    reduce_scatter x1, waiting for transfers between devices, body(): lax.psum_scatter(down_weight_term, ('seq', 'sub'), scatter_dimension=0, t...  249 us
    all_gather x2, waiting for transfers between devices, body(): lax.all_gather(barrier_set[2], ('seq', 'sub'), axis=0, tiled=True)  142 us
    reduce_scatter x1, waiting for transfers between devices, body(): lax.psum_scatter(key_weight_term, ('seq', 'sub'), scatter_dimension=0, ti...  142 us
    reduce_scatter x1, waiting for transfers between devices, body(): lax.psum_scatter(value_weight_term, ('seq', 'sub'), scatter_dimension=0,...  142 us
  transfers between devices with their start and end apart: 32, of which 26 were waited for; matrix products, arithmetic and copies ran while one was open for 18% of the time, Pallas kernels for 0%

commit v1 on v0

v1 whole, which is shorter than its diff:
```python
import functools
import math

import jax
import jax.numpy as jnp
from jax import lax
from jax.experimental import pallas as pl
from jax.experimental.pallas import tpu as pltpu
from jax.sharding import PartitionSpec as P

CAP = 256
LANES = 128
BLOCK = 256

epsilon = 1e-06
rope_base = 10000.0
masked_score = -1e30
highest = lax.Precision.HIGHEST
f32 = jnp.float32
bf16 = jnp.bfloat16
NT = (((1,), (1,)), ((), ()))
TN = (((0,), (0,)), ((), ()))
NN = (((1,), (0,)), ((), ()))
BOTH = ("seq", "sub")


def dot(a, b, dims=NN):
    return lax.dot_general(a, b, dims, preferred_element_type=f32)


def inv_rms(values):
    return lax.rsqrt(jnp.mean(values * values, -1, keepdims=True) + epsilon)


def norm_back(normed_hat, inverse, grad_hat):
    return inverse * (grad_hat - normed_hat * jnp.mean(normed_hat * grad_hat, -1, keepdims=True))


def round_keep(values):
    return lax.optimization_barrier(values.astype(bf16)).astype(f32)


def shift_pairs(count, step):
    return [(i, (i + step) % count) for i in range(count)]


def gather_sub(x):
    count = lax.axis_size("sub")
    me = lax.axis_index("sub")
    rows = x.shape[0]
    rest = (0,) * (x.ndim - 1)
    out = lax.dynamic_update_slice(
        jnp.zeros((count * rows,) + x.shape[1:], x.dtype), x, (me * rows,) + rest
    )
    for step in range(1, count):
        got = lax.ppermute(x, "sub", shift_pairs(count, step))
        out = lax.dynamic_update_slice(out, got, ((me - step) % count * rows,) + rest)
    return out


def exchange_sub(x):
    count = lax.axis_size("sub")
    me = lax.axis_index("sub")
    out = x
    for step in range(1, count):
        block = lax.dynamic_slice_in_dim(x, (me + step) % count, 1, 0)
        got = lax.ppermute(block, "sub", shift_pairs(count, step))
        out = lax.dynamic_update_slice_in_dim(out, got, (me - step) % count, 0)
    return out


def scatter_sub(x):
    count = lax.axis_size("sub")
    me = lax.axis_index("sub")
    rows = x.shape[0] // count
    total = lax.dynamic_slice_in_dim(x, me * rows, rows, 0)
    low = x.astype(bf16)
    for step in range(1, count):
        block = lax.dynamic_slice_in_dim(low, (me + step) % count * rows, rows, 0)
        got = lax.ppermute(block, "sub", shift_pairs(count, step))
        total = total + got.astype(f32)
    return total


def pad_lanes(x):
    extra = -x.shape[-1] % LANES
    if extra == 0:
        return x
    return jnp.pad(x, [(0, 0)] * (x.ndim - 1) + [(0, extra)])


def attn_fwd_kernel(scale, rng_ref, lo_ref, hi_ref, q_ref, k_ref, v_ref, o_ref, lse_ref):
    rows = q_ref.shape[0]
    half = LANES // 2
    lane = lax.broadcasted_iota(jnp.int32, (BLOCK, LANES), 1)
    for qb in range(rows // BLOCK):
        cut = slice(qb * BLOCK, (qb + 1) * BLOCK)
        q = q_ref[cut, :]
        zero = jnp.zeros_like(q)
        qs = (jnp.where(lane < half, q, zero), jnp.where(lane >= half, q, zero))
        lo = lo_ref[0:1, cut]
        hi = hi_ref[0:1, cut]

        def step(i, carry):
            stats, acc = carry
            at = pl.ds(pl.multiple_of(i * BLOCK, BLOCK), BLOCK)
            k = k_ref[at, :]
            v = v_ref[at, :]
            index = i * BLOCK + lax.broadcasted_iota(jnp.int32, (BLOCK, BLOCK), 0)
            allowed = (index >= lo) & (index < hi)
            new_stats = []
            parts = []
            for h in range(2):
                top, norm = stats[h]
                scores = jnp.where(allowed, dot(k, qs[h], NT) * scale, masked_score)
                new_top = jnp.maximum(top, jnp.max(scores, 0, keepdims=True))
                probs = jnp.exp(scores - new_top)
                factor = jnp.exp(top - new_top)
                norm = norm * factor + jnp.sum(probs, 0, keepdims=True)
                out = dot(v, probs.astype(bf16), TN)[h * half : (h + 1) * half, :]
                parts.append(acc[h * half : (h + 1) * half, :] * factor + out)
                new_stats.append((new_top, norm))
            return tuple(new_stats), jnp.concatenate(parts, 0)

        first = (jnp.full((1, BLOCK), masked_score, f32), jnp.zeros((1, BLOCK), f32))
        stats, acc = lax.fori_loop(
            rng_ref[qb, 0],
            rng_ref[qb, 1],
            step,
            ((first, first), jnp.zeros((LANES, BLOCK), f32)),
        )
        for h in range(2):
            top, norm = stats[h]
            o_ref[h * half : (h + 1) * half, cut] = acc[h * half : (h + 1) * half, :] / norm
            lse_ref[h : h + 1, cut] = top + jnp.log(norm)


def attn_bwd_kernel(
    scale, rng_ref, lo_ref, hi_ref, q_ref, k_ref, v_ref, g_ref, o_ref, lse_ref, dq_ref, dkv_ref, dk, dv
):
    rows = q_ref.shape[0]
    half = LANES // 2
    lane = lax.broadcasted_iota(jnp.int32, (BLOCK, LANES), 1)
    keys = k_ref.shape[0]

    def clear(i, unused):
        at = pl.ds(pl.multiple_of(i * BLOCK, BLOCK), BLOCK)
        dk[at, :] = jnp.zeros((BLOCK, LANES), f32)
        dv[at, :] = jnp.zeros((BLOCK, LANES), f32)
        return unused

    lax.fori_loop(0, keys // BLOCK, clear, 0)
    for qb in range(rows // BLOCK):
        cut = slice(qb * BLOCK, (qb + 1) * BLOCK)
        q = q_ref[cut, :]
        g = g_ref[cut, :]
        zero = jnp.zeros_like(q)
        qs = (jnp.where(lane < half, q, zero), jnp.where(lane >= half, q, zero))
        gs = (jnp.where(lane < half, g, zero), jnp.where(lane >= half, g, zero))
        product = jnp.transpose(g.astype(f32)) * o_ref[:, cut]
        deltas = [
            jnp.sum(product[h * half : (h + 1) * half, :], 0, keepdims=True) for h in range(2)
        ]
        logs = [lse_ref[h : h + 1, cut] for h in range(2)]
        lo = lo_ref[0:1, cut]
        hi = hi_ref[0:1, cut]

        def step(i, dq):
            at = pl.ds(pl.multiple_of(i * BLOCK, BLOCK), BLOCK)
            k = k_ref[at, :]
            v = v_ref[at, :]
            index = i * BLOCK + lax.broadcasted_iota(jnp.int32, (BLOCK, BLOCK), 0)
            allowed = (index >= lo) & (index < hi)
            dk_new = dk[at, :]
            dv_new = dv[at, :]
            terms = []
            for h in range(2):
                scores = dot(k, qs[h], NT) * scale
                probs = jnp.where(allowed, jnp.exp(scores - logs[h]), 0.0)
                prob_grad = dot(v, gs[h], NT)
                score_grad = (probs * (prob_grad - deltas[h])).astype(bf16)
                dv_new = dv_new + dot(probs.astype(bf16), gs[h])
                dk_new = dk_new + dot(score_grad, qs[h])
                terms.append(dot(score_grad, k, TN))
            dk[at, :] = dk_new
            dv[at, :] = dv_new
            return dq + jnp.where(lane < half, terms[0], terms[1])

        dq = lax.fori_loop(
            rng_ref[qb, 0], rng_ref[qb, 1], step, jnp.zeros((BLOCK, LANES), f32)
        )
        dq_ref[cut, :] = dq * scale

    def flush(i, unused):
        at = pl.ds(pl.multiple_of(i * BLOCK, BLOCK), BLOCK)
        dkv_ref[at, 0:LANES] = (dk[at, :] * scale).astype(bf16)
        dkv_ref[at, LANES : 2 * LANES] = dv[at, :].astype(bf16)
        return unused

    lax.fori_loop(0, keys // BLOCK, flush, 0)


def column(rows, width=LANES, shift=0):
    return pl.BlockSpec((rows, width), lambda p: (0, p + shift))


def whole(array):
    return pl.BlockSpec(array.shape, lambda p: (0, 0))


def attn_forward(name, scale, spans, q, kv):
    lo, hi, rng = spans
    rows, width = q.shape
    keys = kv.shape[0]
    pairs = width // LANES
    return pl.pallas_call(
        functools.partial(attn_fwd_kernel, scale),
        grid=(pairs,),
        in_specs=[
            pl.BlockSpec(memory_space=pltpu.SMEM),
            whole(lo),
            whole(hi),
            column(rows),
            column(keys),
            column(keys, shift=pairs),
        ],
        out_specs=[
            pl.BlockSpec((LANES, rows), lambda p: (p, 0)),
            pl.BlockSpec((8, rows), lambda p: (p, 0)),
        ],
        out_shape=[
            jax.ShapeDtypeStruct((width, rows), f32),
            jax.ShapeDtypeStruct((pairs * 8, rows), f32),
        ],
        compiler_params=pltpu.CompilerParams(vmem_limit_bytes=56 * 1024 * 1024),
        cost_estimate=pl.CostEstimate(
            flops=4 * rows * keys * width // 2,
            bytes_accessed=4 * keys * width,
            transcendentals=rows * keys * width // 128,
        ),
        name=name,
    )(rng, lo, hi, q, kv, kv)


def attn_backward(name, scale, spans, q, kv, grad, out, lse):
    lo, hi, rng = spans
    rows, width = q.shape
    keys = kv.shape[0]
    pairs = width // LANES
    return pl.pallas_call(
        functools.partial(attn_bwd_kernel, scale),
        grid=(pairs,),
        in_specs=[
            pl.BlockSpec(memory_space=pltpu.SMEM),
            whole(lo),
            whole(hi),
            column(rows),
            column(keys),
            column(keys, shift=pairs),
            column(rows),
            pl.BlockSpec((LANES, rows), lambda p: (p, 0)),
            pl.BlockSpec((8, rows), lambda p: (p, 0)),
        ],
        out_specs=[column(rows), column(keys, 2 * LANES)],
        out_shape=[
            jax.ShapeDtypeStruct((rows, width), f32),
            jax.ShapeDtypeStruct((keys, 2 * width), bf16),
        ],
        scratch_shapes=[pltpu.VMEM((keys, LANES), f32), pltpu.VMEM((keys, LANES), f32)],
        compiler_params=pltpu.CompilerParams(vmem_limit_bytes=56 * 1024 * 1024),
        cost_estimate=pl.CostEstimate(
            flops=10 * rows * keys * width // 2,
            bytes_accessed=8 * keys * width,
            transcendentals=rows * keys * width // 128,
        ),
        name=name,
    )(rng, lo, hi, q, kv, kv, grad, out, lse)


def split_pairs(x, width):
    rows = x.shape[0]
    shaped = x.reshape(rows, -1, 2, LANES)
    return (
        shaped[:, :, 0].reshape(rows, -1)[:, :width],
        shaped[:, :, 1].reshape(rows, -1)[:, :width],
    )


def make_spans(lo, hi):
    first = lo[::BLOCK] // BLOCK
    last = (hi[BLOCK - 1 :: BLOCK] + BLOCK - 1) // BLOCK
    return lo[None, :], hi[None, :], jnp.stack([first, last], 1)


def rope_tables(positions, head_dim, width):
    pair_total = head_dim // 2
    frame_pairs = pair_total // 4
    height_pairs = (pair_total - frame_pairs) // 2
    width_pairs = pair_total - frame_pairs - height_pairs
    pieces = []
    for axis_id, pair_count in enumerate((frame_pairs, height_pairs, width_pairs)):
        frequency = rope_base ** (-jnp.arange(pair_count, dtype=f32) / pair_count)
        row = [jnp.zeros((n,), f32) for n in (frame_pairs, height_pairs, width_pairs)]
        row[axis_id] = frequency
        pieces.append(jnp.tile(jnp.repeat(jnp.concatenate(row), 2), LANES // head_dim))
    where = positions.astype(f32)
    angles = sum(where[:, i : i + 1] * pieces[i][None, :] for i in range(3))
    odd = lax.broadcasted_iota(jnp.int32, angles.shape, 1) % 2 == 1
    cosine = jnp.cos(angles)
    sine = jnp.sin(angles)
    sine = jnp.where(odd, sine, -sine)
    copies = -(-width // LANES)
    return (
        jnp.concatenate([cosine] * copies, 1)[:, :width],
        jnp.concatenate([sine] * copies, 1)[:, :width],
    )


def swap_pairs(x):
    odd = lax.broadcasted_iota(jnp.int32, x.shape, 1) % 2 == 1
    return jnp.where(odd, jnp.roll(x, 1, 1), jnp.roll(x, -1, 1))


def clip_index(token_index, clip_lengths):
    bounds = jnp.cumsum(clip_lengths)
    return jnp.sum((token_index[:, None] >= bounds[None, :]).astype(jnp.int32), 1)


def embed(value, size, start, axis=-1):
    axis = axis % value.ndim
    shape = list(value.shape)
    shape[axis] = size
    return lax.dynamic_update_slice_in_dim(jnp.zeros(shape, value.dtype), value, start, axis)


def body(
    video,
    conditioning,
    captions,
    clip_lengths,
    cap_lengths,
    positions,
    ada_weight,
    ada_bias,
    query_weight,
    key_weight,
    value_weight,
    out_weight,
    text_key_weight,
    text_value_weight,
    gate_weight,
    up_weight,
    down_weight,
    attn_gain,
    query_gain,
    key_gain,
    text_key_gain,
    attn_out_gain,
    ffn_gain,
    ffn_out_gain,
    cross_gate,
    cotangent,
):
    num_sub = lax.axis_size("sub")
    num_seq = lax.axis_size("seq")
    tok_rows, model_width = video.shape
    heads_total = cross_gate.shape[0]
    head_dim = model_width // heads_total
    heads_local = heads_total // num_sub
    local_width = heads_local * head_dim
    score_scale = 1.0 / math.sqrt(head_dim)
    sub_index = lax.axis_index("sub")
    seq_index = lax.axis_index("seq")
    device_index = seq_index * num_sub + sub_index
    group_rows = tok_rows * num_sub
    clip_count = clip_lengths.shape[0]
    clip_range = jnp.arange(clip_count, dtype=jnp.int32)
    rows = query_weight.shape[0]
    text_rows = text_key_weight.shape[0]
    hidden_rows = down_weight.shape[0]
    hidden_local = num_seq * hidden_rows
    lanes = local_width + (-local_width % LANES)

    video_group = gather_sub(video)
    positions_group = gather_sub(positions)

    def by_sub(weight):
        return weight.reshape(weight.shape[0], num_sub, -1)

    qkv_shard = jnp.concatenate([by_sub(w) for w in (query_weight, key_weight, value_weight)], 2)
    qkv_full = lax.all_gather(
        exchange_sub(qkv_shard.transpose(1, 0, 2)).reshape(num_sub * rows, 3 * local_width),
        "seq", axis=0, tiled=True,
    )
    text_shard = jnp.concatenate([by_sub(w) for w in (text_key_weight, text_value_weight)], 2)
    text_full = lax.all_gather(
        exchange_sub(text_shard.transpose(1, 0, 2)).reshape(num_sub * text_rows, 2 * local_width),
        "seq", axis=0, tiled=True,
    )

    def hidden_by_sub(weight):
        shaped = weight.reshape(rows, num_seq, num_sub, hidden_rows).transpose(2, 0, 1, 3)
        return shaped.reshape(num_sub, rows, hidden_local)

    ffn_shard = jnp.concatenate([hidden_by_sub(gate_weight), hidden_by_sub(up_weight)], 2)
    out_move = [
        (j, j % num_seq * num_sub + j // num_seq) for j in range(num_seq * num_sub)
    ]
    out_full = lax.all_gather(
        lax.ppermute(out_weight, BOTH, out_move), "seq", axis=0, tiled=True
    )
    ffn_full = lax.all_gather(
        exchange_sub(ffn_shard).reshape(num_sub * rows, 2 * hidden_local),
        "seq", axis=0, tiled=True,
    )
    down_full = lax.all_gather(down_weight, "seq", axis=0, tiled=True)

    cond_float = conditioning.astype(f32)
    cond_act = jax.nn.silu(cond_float).astype(bf16)
    cond_rows, mod_width = ada_weight.shape
    cond_slice = lax.dynamic_slice_in_dim(cond_act, device_index * cond_rows, cond_rows, 1)
    bias_rows = ada_bias.shape[0]
    mod_part = dot(cond_slice, ada_weight) + embed(
        ada_bias.astype(f32)[None], mod_width, device_index * bias_rows
    )
    gain_shard = jnp.stack(
        [attn_gain, query_gain, key_gain, text_key_gain, attn_out_gain, ffn_gain, ffn_out_gain]
    ).astype(f32)
    modulation, gains = lax.psum(
        (mod_part, embed(gain_shard, model_width, device_index * rows)), BOTH
    )
    attn_gain_f = gains[0]
    attn_out_f = gains[4]
    ffn_gain_f = gains[5]
    ffn_out_f = gains[6]

    def own_columns(value):
        return lax.dynamic_slice_in_dim(value, sub_index * local_width, local_width, 0)

    query_gain_f = own_columns(gains[1])
    key_gain_f = own_columns(gains[2])
    text_key_gain_f = own_columns(gains[3])

    token_index = device_index * tok_rows + jnp.arange(tok_rows, dtype=jnp.int32)
    token_clip = clip_index(token_index, clip_lengths)
    clip_onehot = (token_clip[:, None] == clip_range[None, :]).astype(f32)
    per_token = jnp.dot(clip_onehot, modulation, precision=highest)
    attn_scale = per_token[:, :model_width]
    attn_gate = per_token[:, model_width : 2 * model_width]
    ffn_scale = per_token[:, 2 * model_width : 3 * model_width]
    ffn_gate = per_token[:, 3 * model_width :]

    group_index = seq_index * group_rows + jnp.arange(group_rows, dtype=jnp.int32)
    group_clip = clip_index(group_index, clip_lengths)
    group_hot = group_clip[:, None] == clip_range[None, :]

    def of_clip(values):
        return jnp.sum(jnp.where(group_hot, values[None, :], 0), 1)

    clip_ends = jnp.cumsum(clip_lengths)
    self_spans = make_spans(of_clip(clip_ends - clip_lengths), of_clip(clip_ends))
    cross_spans = make_spans(group_clip * CAP, group_clip * CAP + of_clip(cap_lengths))

    group_scale = jnp.dot(group_hot.astype(f32), modulation[:, :model_width], precision=highest)
    video_g = video_group.astype(f32)
    normed = (video_g * inv_rms(video_g) * (attn_gain_f * (1.0 + group_scale))).astype(bf16)
    qkv_pre = dot(normed, qkv_full)
    query_pre = qkv_pre[:, :local_width]
    key_pre = qkv_pre[:, local_width : 2 * local_width]
    values_own = qkv_pre[:, 2 * local_width :].astype(bf16)

    cap_shard = captions.shape[0]
    cap_rows = cap_shard // num_seq
    cap_group = gather_sub(lax.dynamic_slice_in_dim(captions, seq_index * cap_rows, cap_rows, 0))
    text_pre = dot(cap_group, text_full)
    text_key_pre = text_pre[:, :local_width]

    def sum_sub(*parts):
        return lax.psum(jnp.stack(parts), "sub")

    text_square = sum_sub(jnp.sum(text_key_pre * text_key_pre, 1))
    text_inv = lax.rsqrt(text_square[0] / model_width + epsilon)[:, None]
    text_hat = text_key_pre * text_inv
    text_keys = (text_hat * text_key_gain_f).astype(bf16)
    text_values = text_pre[:, local_width:].astype(bf16)
    text_kv = lax.all_gather(
        jnp.concatenate([pad_lanes(text_keys), pad_lanes(text_values)], 1), "seq", axis=0, tiled=True
    )
    text_kv = text_kv.reshape(num_seq, num_sub, cap_rows, 2 * lanes).transpose(1, 0, 2, 3)
    text_kv = text_kv.reshape(num_sub * cap_shard, 2 * lanes)

    squares = sum_sub(jnp.sum(query_pre * query_pre, 1), jnp.sum(key_pre * key_pre, 1))
    inverses = lax.rsqrt(squares / model_width + epsilon)
    query_inv = inverses[0][:, None]
    key_inv = inverses[1][:, None]
    query_hat = query_pre * query_inv
    key_hat = key_pre * key_inv
    cosine, sine = rope_tables(positions_group, head_dim, local_width)

    def turn(value):
        return value * cosine + swap_pairs(value) * sine

    def turn_back(value):
        return value * cosine - swap_pairs(value) * sine

    queries = pad_lanes(turn(query_hat * query_gain_f).astype(bf16))
    keys_own = turn(key_hat * key_gain_f).astype(bf16)
    kv_all = lax.all_gather(
        jnp.concatenate([pad_lanes(keys_own), pad_lanes(values_own)], 1), "seq", axis=0, tiled=True
    )

    cross_t, cross_lse = attn_forward("cross_fwd", score_scale, cross_spans, queries, text_kv)
    self_t, self_lse = attn_forward("self_fwd", score_scale, self_spans, queries, kv_all)

    gate_tanh = jnp.tanh(cross_gate.astype(f32))
    own_gate = lax.dynamic_slice_in_dim(gate_tanh, sub_index * heads_local, heads_local, 0)
    gate_rows = jnp.repeat(own_gate, head_dim)
    mixed = (
        (
            self_t[:local_width].astype(bf16).astype(f32)
            + gate_rows[:, None] * cross_t[:local_width]
        )
        .astype(bf16)
        .T
    )
    projected = scatter_sub(dot(mixed, out_full))
    proj_inv = inv_rms(projected)
    proj_hat = projected * proj_inv
    attn_tanh = jnp.tanh(attn_gate)
    video_float = video.astype(f32)
    hidden_state = video_float + attn_tanh * proj_hat * attn_out_f
    hidden_inv = inv_rms(hidden_state)
    hidden_hat = hidden_state * hidden_inv
    ffn_mult = ffn_gain_f * (1.0 + ffn_scale)
    ffn_in = gather_sub((hidden_hat * ffn_mult).astype(bf16))
    ffn_pre = dot(ffn_in, ffn_full)
    gate_pre = ffn_pre[:, :hidden_local]
    up_pre = ffn_pre[:, hidden_local:]
    activated = (jax.nn.silu(gate_pre) * up_pre).astype(bf16)
    down_out = scatter_sub(dot(activated, down_full))
    down_inv = inv_rms(down_out)
    down_hat = down_out * down_inv
    ffn_tanh = jnp.tanh(ffn_gate)
    block_out = (hidden_state + ffn_tanh * down_hat * ffn_out_f).astype(bf16)

    grad_out = cotangent.astype(f32)
    down_grad = gather_sub(
        norm_back(down_hat, down_inv, grad_out * ffn_tanh * ffn_out_f).astype(bf16)
    )
    act_grad = dot(down_grad, down_full, NT)
    gate_sig = jax.nn.sigmoid(gate_pre)
    gate_grad = act_grad * up_pre * gate_sig * (1.0 + gate_pre * (1.0 - gate_sig))
    up_grad = act_grad * jax.nn.silu(gate_pre)
    ffn_grad = jnp.concatenate([gate_grad.astype(bf16), up_grad.astype(bf16)], 1)
    ffn_in_grad = scatter_sub(dot(ffn_grad, ffn_full, NT))
    hidden_grad = grad_out + norm_back(hidden_hat, hidden_inv, ffn_in_grad * ffn_mult)
    proj_grad = gather_sub(
        norm_back(proj_hat, proj_inv, hidden_grad * attn_tanh * attn_out_f).astype(bf16)
    )
    mixed_grad = dot(proj_grad, out_full, NT).astype(bf16)

    def reduce_seq(term):
        return lax.psum_scatter(term.astype(bf16), "seq", scatter_dimension=0, tiled=True)

    down_weight_grad = reduce_seq(dot(activated, down_grad, TN)).astype(f32)
    ffn_weight_sum = reduce_seq(dot(ffn_in, ffn_grad, TN))
    out_weight_sum = reduce_seq(dot(mixed, proj_grad, TN))

    mixed_grad_f = mixed_grad.astype(f32)
    gate_terms = jnp.sum(mixed_grad_f.T * cross_t[:local_width], 1)
    cross_gate_part = jnp.sum(gate_terms.reshape(heads_local, head_dim), 1) * (
        1.0 - own_gate * own_gate
    )
    cross_out_grad = (mixed_grad_f * gate_rows).astype(bf16)
    query_cross, text_terms = attn_backward(
        "cross_bwd", score_scale, cross_spans, queries, text_kv, pad_lanes(cross_out_grad), cross_t, cross_lse
    )
    text_terms = text_terms.reshape(num_sub, num_seq, cap_rows, -1).transpose(1, 0, 2, 3)
    text_sum = reduce_seq(text_terms.reshape(num_sub * cap_shard, -1))
    query_self, kv_terms = attn_backward(
        "self_bwd", score_scale, self_spans, queries, kv_all, pad_lanes(mixed_grad), self_t, self_lse
    )
    key_grad, value_grad = split_pairs(reduce_seq(kv_terms), local_width)

    text_key_low, text_value_low = split_pairs(text_sum, local_width)
    text_key_low = text_key_low.astype(f32)
    text_key_gain_part = jnp.sum(text_key_low * text_hat, 0)
    text_grad_hat = text_key_low * text_key_gain_f
    text_mean = sum_sub(jnp.sum(text_hat * text_grad_hat, 1))[0][:, None] / model_width
    text_key_pre_grad = text_inv * (text_grad_hat - text_hat * text_mean)
    text_grad = jnp.concatenate([text_key_pre_grad.astype(bf16), text_value_low], 1)
    text_weight_sum = reduce_seq(dot(cap_group, text_grad, TN))
    caption_rows_grad = scatter_sub(dot(text_grad, text_full, NT))
    caption_grad = lax.all_gather(
        caption_rows_grad.astype(bf16), "seq", axis=0, tiled=True
    ).astype(f32)

    query_norm_grad = turn_back(round_keep((query_self + query_cross)[:, :local_width]))
    key_norm_grad = turn_back(key_grad.astype(f32))
    query_gain_part = jnp.sum(query_norm_grad * query_hat, 0)
    key_gain_part = jnp.sum(key_norm_grad * key_hat, 0)
    query_grad_hat = query_norm_grad * query_gain_f
    key_grad_hat = key_norm_grad * key_gain_f
    means = sum_sub(
        jnp.sum(query_hat * query_grad_hat, 1), jnp.sum(key_hat * key_grad_hat, 1)
    ) / model_width
    query_pre_grad = query_inv * (query_grad_hat - query_hat * means[0][:, None])
    key_pre_grad = key_inv * (key_grad_hat - key_hat * means[1][:, None])
    qkv_grad = jnp.concatenate(
        [query_pre_grad.astype(bf16), key_pre_grad.astype(bf16), value_grad], 1
    )
    normed_grad = scatter_sub(dot(qkv_grad, qkv_full, NT))
    qkv_weight_sum = reduce_seq(dot(normed, qkv_grad, TN))

    video_inv = inv_rms(video_float)
    video_hat = video_float * video_inv
    attn_mult = attn_gain_f * (1.0 + attn_scale)
    video_grad = hidden_grad + norm_back(video_hat, video_inv, normed_grad * attn_mult)

    token_mod_grad = jnp.concatenate(
        [
            normed_grad * video_hat * attn_gain_f,
            hidden_grad * proj_hat * attn_out_f * (1.0 - attn_tanh * attn_tanh),
            ffn_in_grad * hidden_hat * ffn_gain_f,
            grad_out * down_hat * ffn_out_f * (1.0 - ffn_tanh * ffn_tanh),
        ],
        1,
    )
    mod_grad_part = jnp.einsum("tc,tm->cm", clip_onehot, token_mod_grad, precision=highest)
    own_parts = embed(
        jnp.stack([query_gain_part, key_gain_part, text_key_gain_part]),
        model_width,
        sub_index * local_width,
    )
    gain_part = jnp.concatenate(
        [
            jnp.stack(
                [
                    jnp.sum(normed_grad * video_hat * (1.0 + attn_scale), 0),
                    jnp.sum(hidden_grad * attn_tanh * proj_hat, 0),
                    jnp.sum(ffn_in_grad * hidden_hat * (1.0 + ffn_scale), 0),
                    jnp.sum(grad_out * ffn_tanh * down_hat, 0),
                ]
            ),
            own_parts,
        ],
        0,
    )
    mod_sum, gain_sum, gate_sum = lax.psum(
        (mod_grad_part, gain_part, embed(cross_gate_part, heads_total, sub_index * heads_local)),
        BOTH,
    )
    own_gains = lax.dynamic_slice_in_dim(gain_sum, device_index * rows, rows, 1)
    mod_low = mod_sum.astype(bf16)
    ada_bias_grad = jnp.sum(
        lax.dynamic_slice_in_dim(mod_low.astype(f32), device_index * bias_rows, bias_rows, 1), 0
    )
    ada_weight_grad = dot(cond_slice, mod_low, TN)
    cond_sig = jax.nn.sigmoid(cond_float)
    cond_part = embed(
        dot(mod_low, ada_weight, NT), conditioning.shape[1], device_index * cond_rows
    )
    cond_grad = (
        lax.psum(lax.psum(cond_part, "sub"), "seq")
        * cond_sig
        * (1.0 + cond_float * (1.0 - cond_sig))
    )

    def from_sub(term, count):
        shaped = exchange_sub(term.reshape(num_sub, -1, term.shape[1])).astype(f32)
        width = term.shape[1] // count
        return [shaped[:, :, i * width : (i + 1) * width] for i in range(count)]

    def join_columns(blocks):
        return blocks.transpose(1, 0, 2).reshape(blocks.shape[1], -1)

    def join_hidden(blocks):
        shaped = blocks.reshape(num_sub, rows, num_seq, hidden_rows).transpose(1, 2, 0, 3)
        return shaped.reshape(rows, -1)

    query_weight_grad, key_weight_grad, value_weight_grad = (
        join_columns(b) for b in from_sub(qkv_weight_sum, 3)
    )
    text_key_weight_grad, text_value_weight_grad = (
        join_columns(b) for b in from_sub(text_weight_sum, 2)
    )
    gate_weight_grad, up_weight_grad = (join_hidden(b) for b in from_sub(ffn_weight_sum, 2))
    out_weight_grad = lax.ppermute(
        out_weight_sum, BOTH, [(b, a) for a, b in out_move]
    ).astype(f32)
    return (
        block_out,
        video_grad,
        caption_grad,
        cond_grad,
        ada_weight_grad,
        ada_bias_grad,
        query_weight_grad,
        key_weight_grad,
        value_weight_grad,
        out_weight_grad,
        text_key_weight_grad,
        text_value_weight_grad,
        gate_weight_grad,
        up_weight_grad,
        down_weight_grad,
        own_gains[0],
        own_gains[4],
        own_gains[5],
        own_gains[6],
        own_gains[1],
        own_gains[2],
        own_gains[3],
        gate_sum,
    )


def solution(mesh):
    placed = (
        P(("seq", "sub"), None),
        P(),
        P("sub", None),
        P(),
        P(),
        P(("seq", "sub"), None),
        P(("seq", "sub"), None),
        P(("seq", "sub")),
        P(("seq", "sub"), None),
        P(("seq", "sub"), None),
        P(("seq", "sub"), None),
        P(("seq", "sub"), None),
        P(("seq", "sub"), None),
        P(("seq", "sub"), None),
        P(("seq", "sub"), None),
        P(("seq", "sub"), None),
        P(("seq", "sub"), None),
        P(("seq", "sub")),
        P(("seq", "sub")),
        P(("seq", "sub")),
        P(("seq", "sub")),
        P(("seq", "sub")),
        P(("seq", "sub")),
        P(("seq", "sub")),
        P(),
        P(("seq", "sub"), None),
    )
    return jax.shard_map(
        body,
        mesh=mesh,
        in_specs=placed,
        out_specs=(
            P(("seq", "sub"), None),
            P(("seq", "sub"), None),
            P("sub", None),
            P(),
            P(("seq", "sub"), None),
            P(("seq", "sub")),
            P(("seq", "sub"), None),
            P(("seq", "sub"), None),
            P(("seq", "sub"), None),
            P(("seq", "sub"), None),
            P(("seq", "sub"), None),
            P(("seq", "sub"), None),
            P(("seq", "sub"), None),
            P(("seq", "sub"), None),
            P(("seq", "sub"), None),
            P(("seq", "sub")),
            P(("seq", "sub")),
            P(("seq", "sub")),
            P(("seq", "sub")),
            P(("seq", "sub")),
            P(("seq", "sub")),
            P(("seq", "sub")),
            P(),
        ),
        check_vma=False,
    )
```

time: 3350 us -> 1050 us (0.31)
  waiting for transfers between devices: 2440 us -> 369 us
  matrix products: 440 us -> 78 us
  starting transfers between devices: 17.9 us -> 143 us
  Pallas kernels: 0 us -> 70.5 us
  other arithmetic: 117 us -> 58.3 us
  local copies, waits for them, and re-layouts: 155 us -> 108 us
  blocking collectives: 153 us -> 190 us
    reduce_scatter x12 -> x7, waiting for transfers between devices: 1690 us -> 90.9 us  [reduce_seq(): lax.psum_scatter(term.astype(bf16), 'seq', scatter_dimension=0, tiled=True)]
    all_gather x15 -> x8, waiting for transfers between devices: 652 us -> 16.9 us  [the longest x1 16.6 us: body(): lax.all_gather(jnp.concatenate([pad_lanes(keys_own), pad_lanes(values_own...]
    dot_general x63 -> x19, matrix products: 418 us -> 74.7 us  [the longest x18 70.3 us: dot(): return lax.dot_general(a, b, dims, preferred_element_type=f32)]
    ppermute x0 -> x53, waiting for transfers between devices: none -> 243 us  [the longest x15 110 us: scatter_sub(): got = lax.ppermute(block, 'sub', shift_pairs(count, step))]
    psum x1 -> x6, blocking collectives: 43.3 us -> 190 us  [the longest x1 68.1 us: body(): lax.psum((mod_part, embed(gain_shard, model_width, device_index * rows)),...]
    ppermute x0 -> x53, starting transfers between devices: none -> 141 us  [the longest x18 52.8 us: exchange_sub(): got = lax.ppermute(block, 'sub', shift_pairs(count, step))]
    unnamed x29 -> x16, waiting for transfers between devices: 75.7 us -> 0.78 us
    pallas_call x0 -> x4, Pallas kernels: none -> 70.5 us  [the longest x2 39.1 us: attn_backward(): pl.pallas_call(functools.partial(attn_bwd_kernel, scale), grid=(pairs,),...]
  transfers between devices with their start and end apart: 32 -> 69, of which waited for: 26 -> 34; matrix products, arithmetic and copies ran while one was open for 18% -> 20% of each run, Pallas kernels for 0% -> 6%
where the time goes in v1:
time: 1050 us; the launch traced here: 1030 us
  waiting for transfers between devices  369 us (35%)
  blocking collectives  190 us (18%)
  starting transfers between devices  143 us (14%)
  local copies, waits for them, and re-layouts  108 us (10%)
  matrix products  78 us (7%)
  Pallas kernels  70.5 us (7%)
  other arithmetic  58.3 us (6%)
  between operations  18.4 us (2%)
    ppermute x15, waiting for transfers between devices, scatter_sub(): got = lax.ppermute(block, 'sub', shift_pairs(count, step))  110 us
    reduce_scatter x7, waiting for transfers between devices, reduce_seq(): lax.psum_scatter(term.astype(bf16), 'seq', scatter_dimension=0, tiled=True)  90.9 us
    ppermute x18, waiting for transfers between devices, gather_sub(): got = lax.ppermute(x, 'sub', shift_pairs(count, step))  72.7 us
    dot_general x18, matrix products, dot(): return lax.dot_general(a, b, dims, preferred_element_type=f32)  70.3 us
    psum x1, blocking collectives, body(): lax.psum((mod_part, embed(gain_shard, model_width, device_index * rows)),...  68.1 us
    ppermute x18, waiting for transfers between devices, exchange_sub(): got = lax.ppermute(block, 'sub', shift_pairs(count, step))  59.5 us
    ppermute x18, starting transfers between devices, exchange_sub(): got = lax.ppermute(block, 'sub', shift_pairs(count, step))  52.8 us
    psum x1, blocking collectives, body(): lax.psum((mod_grad_part, gain_part, embed(cross_gate_part, heads_total, s...  50.1 us
  transfers between devices with their start and end apart: 69, of which 34 were waited for; matrix products, arithmetic and copies ran while one was open for 20% of the time, Pallas kernels for 6%

profile of v1, /device:TPU:0, one launch (start us, length us, event | category | flops | bytes accessed | tf_op | source)
XLA Modules:
  0.0 1034.3 jit_solution(14682776700912660189)
XLA Ops:
  25.0 7.4 collective-permute-done.4
  49.3 6.8 collective-permute-done.13
  72.6 68.1 %psum.78 = f32[7,1536]{1,0:T(8,128)} all-reduce(f32[7,1536]{1,0:T(8,128)} %dynamic_update_slice.147), channel_id=1, replica_groups=mesh['seq'=8,'sub'=4] {'seq','sub'}, use_global_device_ids=true, to_apply=%region_7.8 | all-reduce | flops 10752 | bytes 86016 | tf_op jit(solution)/shard_map/psum | solution.py:429
  157.7 17.8 %all-reduce.7.cloned.1.call-done = f32[5,6144]{1,0:T(8,128)} async-done(((f32[5,6144]{1,0:T(8,128)}), f32[5,6144]{1,0:T(8,128)}) %all-reduce.7.cloned.1.call-update) | async-done | bytes 122896 | tf_op jit(solution)/shard_map/psum | solution.py:429
  190.0 13.0 %all-reduce.3 = (f32[2,512]{1,0:T(2,128)S(1)}, f32[1,160]{1,0:T(1,128)S(1)}) all-reduce(f32[2,512]{1,0:T(2,128)S(1)} %pad_maximum_fusion.14, f32[1,160]{1,0:T(1,128)S(1)} %bitcast.248), channel_id=1, replica_groups=mesh['seq'=8,'sub'=4] {'sub'}, use_global_device_ids=true, to_apply=%region_10.11 | all-reduce | flops 1184 | bytes 9472 | tf_op jit(solution)/shard_map/psum | solution.py:479
  216.7 9.9 collective-permute-start.22
  236.8 7.4 collective-permute-done.23
  254.5 6.6 cross_fwd.1
  261.1 16.6 %all-gather.11.cloned.1.call-done.k_ref.v_ref = bf16[4096,768]{1,0:T(8,128)(2,1)} async-done(((bf16[512,768]{1,0:T(8,128)(2,1)}), bf16[4096,768]{1,0:T(8,128)(2,1)}) %all-gather.11.cloned.1.call-update) | async-done | bytes 6291472 | tf_op jit(solution)/shard_map/all_gather | solution.py:508
  277.8 24.8 %self_fwd.1 = (f32[384,512]{1,0:T(8,128)}, f32[24,512]{1,0:T(8,128)}) custom-call(s32[2,2]{1,0:T(2,128)} %pad_add_fusion.rng_ref, s32[1,512]{1,0:T(1,128)} %bitcast.234, s32[1,512]{1,0:T(1,128)} %bitcast.236, bf16[512,384]{1,0:T(8,128)(2,1)} %fusion.33.q_ref, bf16[4096,768]{1,0:T(8,128)(2,1)} %all-gather.11.cloned.1.call-done.k_ref.v_ref, ...), custom_call_target="tpu_custom_call" | custom-call | flops 1610612736 | bytes 6291456 | tf_op jit(solution)/shard_map/self_fwd/pallas_call | solution.py:216
  313.9 6.6 collective-permute-done.16
  320.5 16.1 %collective-permute-done.17 = bf16[128,1536]{1,0:T(8,128)(2,1)S(1)} collective-permute-done((bf16[128,1536]{1,0:T(8,128)(2,1)S(1)}, bf16[128,1536]{1,0:T(8,128)(2,1)S(1)}, u32[]{:S(2)}, u32[]{:S(2)}) %collective-permute-start.17) | collective-permute-done | bytes 393248 | tf_op jit(solution)/shard_map/ppermute | solution.py:80
  340.0 8.9 collective-permute-start.19
  351.7 8.2 collective-permute-done.19
  360.7 14.8 %collective-permute-done.20 = bf16[128,1536]{1,0:T(8,128)(2,1)S(1)} collective-permute-done((bf16[128,1536]{1,0:T(8,128)(2,1)S(1)}, bf16[128,1536]{1,0:T(8,128)(2,1)S(1)}, u32[]{:S(2)}, u32[]{:S(2)}) %collective-permute-start.20) | collective-permute-done | bytes 393248 | tf_op jit(solution)/shard_map/ppermute | solution.py:56
  377.1 6.0 fusion.108
  390.9 8.2 collective-permute-start.25
  402.0 9.5 collective-permute-done.25
  411.6 15.7 %collective-permute-done.26 = bf16[128,1536]{1,0:T(8,128)(2,1)S(1)} collective-permute-done((bf16[128,1536]{1,0:T(8,128)(2,1)S(1)}, bf16[128,1536]{1,0:T(8,128)(2,1)S(1)}, u32[]{:S(2)}, u32[]{:S(2)}) %collective-permute-start.26) | collective-permute-done | bytes 393248 | tf_op jit(solution)/shard_map/ppermute | solution.py:80
  430.3 8.9 collective-permute-start.28
  441.7 7.6 collective-permute-done.28
  449.3 15.7 %collective-permute-done.29 = bf16[128,1536]{1,0:T(8,128)(2,1)S(1)} collective-permute-done((bf16[128,1536]{1,0:T(8,128)(2,1)S(1)}, bf16[128,1536]{1,0:T(8,128)(2,1)S(1)}, u32[]{:S(2)}, u32[]{:S(2)}) %collective-permute-start.29) | collective-permute-done | bytes 393248 | tf_op jit(solution)/shard_map/ppermute | solution.py:56
  472.0 8.9 collective-permute-start.31
  484.0 9.4 collective-permute-done.31
  493.4 15.6 %collective-permute-done.32 = bf16[128,1536]{1,0:T(8,128)(2,1)S(1)} collective-permute-done((bf16[128,1536]{1,0:T(8,128)(2,1)S(1)}, bf16[128,1536]{1,0:T(8,128)(2,1)S(1)}, u32[]{:S(2)}, u32[]{:S(2)}) %collective-permute-start.32) | collective-permute-done | bytes 393248 | tf_op jit(solution)/shard_map/ppermute | solution.py:80
  514.1 8.9 collective-permute-start.34
  525.5 7.6 collective-permute-done.34
  533.1 15.6 %collective-permute-done.35 = bf16[128,1536]{1,0:T(8,128)(2,1)S(1)} collective-permute-done((bf16[128,1536]{1,0:T(8,128)(2,1)S(1)}, bf16[128,1536]{1,0:T(8,128)(2,1)S(1)}, u32[]{:S(2)}, u32[]{:S(2)}) %collective-permute-start.35) | collective-permute-done | bytes 393248 | tf_op jit(solution)/shard_map/ppermute | solution.py:56
  551.9 8.5 cross_bwd.1
  563.4 30.6 %self_bwd.1 = (f32[512,384]{1,0:T(8,128)}, bf16[4096,768]{1,0:T(8,128)(2,1)}) custom-call(s32[2,2]{1,0:T(2,128)} %pad_add_fusion.rng_ref, s32[1,512]{1,0:T(1,128)} %bitcast.235, s32[1,512]{1,0:T(1,128)} %bitcast.237, bf16[512,384]{1,0:T(8,128)(2,1)} %fusion.33.q_ref, bf16[4096,768]{1,0:T(8,128)(2,1)} %all-gather.11.cloned.1.call-done.k_ref.v_ref, ...), custom_call_target="tpu_custom_call" | custom-call | flops 4026531840 | bytes 12582912 | tf_op jit(solution)/shard_map/self_bwd/pallas_call | solution.py:250
  594.1 8.3 convolution_convert_fusion
  623.1 7.0 reduce-scatter.10.cloned.1.call-done
  631.8 68.3 %reduce-scatter.8.cloned.1.call-done = bf16[512,768]{1,0:T(8,128)(2,1)} async-done(((bf16[4096,768]{1,0:T(8,128)(2,1)}), bf16[512,768]{1,0:T(8,128)(2,1)}) %reduce-scatter.8.cloned.1.call-update) | async-done | bytes 786448 | tf_op jit(solution)/shard_map/reduce_scatter | solution.py:563
  726.8 12.5 %psum.81 = f32[2,512]{1,0:T(2,128)} all-reduce(f32[2,512]{1,0:T(2,128)} %pad_maximum_fusion.15), channel_id=1, replica_groups=mesh['seq'=8,'sub'=4] {'sub'}, use_global_device_ids=true, to_apply=%region_24.25 | all-reduce | flops 1024 | bytes 8192 | tf_op jit(solution)/shard_map/psum | solution.py:479
  760.4 7.6 collective-permute-done.37
  768.0 13.9 %collective-permute-done.38 = bf16[128,1536]{1,0:T(8,128)(2,1)S(1)} collective-permute-done((bf16[128,1536]{1,0:T(8,128)(2,1)S(1)}, bf16[128,1536]{1,0:T(8,128)(2,1)S(1)}, u32[]{:S(2)}, u32[]{:S(2)}) %collective-permute-start.38) | collective-permute-done | bytes 393248 | tf_op jit(solution)/shard_map/ppermute | solution.py:80
  787.2 50.1 %all-reduce.8 = (bf16[5,6144]{1,0:T(8,128)(2,1)}, f32[7,1536]{1,0:T(8,128)}, f32[24]{0:T(128)}) all-reduce(f32[5,6144]{1,0:T(8,128)} %fusion.4, f32[7,1536]{1,0:T(8,128)} %concatenate.93, f32[24]{0:T(128)} %copy-done.94), channel_id=1, replica_groups=mesh['seq'=8,'sub'=4] {'seq','sub'}, use_global_device_ids=true, to_apply=%region_29.30 | all-reduce | flops 41496 | bytes 270528 | tf_op jit(solution)/shard_map/psum | solution.py:649
  840.3 18.5 %all-reduce.2 = (f32[1,160]{1,0:T(1,128)S(1)}, f32[5,1024]{1,0:T(8,128)}) all-reduce(f32[1,160]{1,0:T(1,128)} %bitcast.247, f32[5,1024]{1,0:T(8,128)} %dynamic_update_slice.177), channel_id=1, replica_groups=mesh['seq'=8,'sub'=4] {'sub'}, use_global_device_ids=true, to_apply=%region_28.29 | all-reduce | flops 5280 | bytes 42240 | tf_op jit(solution)/shard_map/psum | solution.py:479
  869.1 8.6 collective-permute-done.40
  877.7 7.5 collective-permute-done.41
  886.2 5.8 convolution_convert_fusion.2
  893.0 6.7 collective-permute-start.50
  911.6 11.1 %collective-permute-start.52 = (bf16[1,48,2048]{2,1,0:T(8,128)(2,1)}, bf16[1,48,2048]{2,1,0:T(8,128)(2,1)S(1)}, u32[]{:S(2)}, u32[]{:S(2)}) collective-permute-start(bf16[1,48,2048]{2,1,0:T(8,128)(2,1)} %get-tuple-element.123), channel_id=1, source_target_pairs={{0,3},{1,0},{2,1},{3,2},{4,7},{5,4},{6,5},{7,6},{8,11},{9,8},{10,9... | collective-permute-start | bytes 589832 | tf_op jit(solution)/shard_map/ppermute | solution.py:67
  938.1 27.6 %psum.85 = f32[5,1024]{1,0:T(8,128)} all-reduce(f32[5,1024]{1,0:T(8,128)} %get-tuple-element.68), channel_id=1, replica_groups=mesh['seq'=8,'sub'=4] {'seq'}, use_global_device_ids=true, to_apply=%region_31.32 | all-reduce | flops 5120 | bytes 40960 | tf_op jit(solution)/shard_map/psum | solution.py:664
  974.3 5.8 collective-permute-done.43
  988.9 15.6 %reduce-scatter.16.cloned.1.call-done = bf16[512,768]{1,0:T(8,128)(2,1)} async-done(((bf16[4096,768]{1,0:T(8,128)(2,1)}), bf16[512,768]{1,0:T(8,128)(2,1)}) %reduce-scatter.16.cloned.1.call-update) | async-done | bytes 786448 | tf_op jit(solution)/shard_map/reduce_scatter | solution.py:563
  1007.1 6.7 collective-permute-done.47
  1018.2 6.1 collective-permute-done.48
  (614 shorter events, 318.7 us)
Async XLA Ops:
  8.1 167.5 %all-reduce.7.cloned.1.call-start = ((), (), s32[]{:S(2)}) async-start(), calls=%async_computation.7 | async-start | bytes 393216 | tf_op jit(solution)/shard_map/psum | solution.py:429
  15.1 17.3 %collective-permute-start.4 = (bf16[1,48,1152]{2,0,1:T(2,128)(2,1)S(1)}, bf16[1,48,1152]{2,0,1:T(2,128)(2,1)S(1)}, u32[]{:S(2)}, u32[]{:S(2)}) collective-permute-start(bf16[1,48,1152]{2,0,1:T(2,128)(2,1)S(1)} %get-tuple-element.153), channel_id=1, source_target_pairs={{0,2},{1,3},{2,0},{3,1},{4,6},{5,7},{6,4},{7,5},{8,10},{9,11},{10,... | collective-permute-start | bytes 331784 | tf_op jit(solution)/shard_map/ppermute | solution.py:67
  20.6 159.4 %all-gather.9.cloned.1.call-start = ((), (), s32[]{:S(2)}) async-start(), calls=%async_computation.8 | async-start | bytes 3981312 | tf_op jit(solution)/shard_map/all_gather | solution.py:391
  36.2 148.7 %all-gather.13.cloned.1.call-start = ((), (), s32[]{:S(2)}) async-start(), calls=%async_computation.10 | async-start | bytes 7077888 | tf_op jit(solution)/shard_map/all_gather | solution.py:396
  57.4 194.2 %all-gather.15.cloned.1.call-start = ((), (), s32[]{:S(2)}) async-start(), calls=%async_computation.11 | async-start | bytes 2211840 | tf_op jit(solution)/shard_map/all_gather | solution.py:486
  58.6 86.5 %collective-permute-start.9 = (bf16[40,4096]{1,0:T(8,128)(2,1)S(1)}, bf16[40,4096]{1,0:T(8,128)(2,1)}, u32[]{:S(2)}, u32[]{:S(2)}) collective-permute-start(bf16[40,4096]{1,0:T(8,128)(2,1)S(1)} %get-tuple-element.92), channel_id=1, source_target_pairs={{0,1},{1,2},{2,3},{3,0},{4,5},{5,6},{6,7},{7,4},{8,9},{9,10},{10,1... | collective-permute-start | bytes 983048 | tf_op jit(solution)/shard_map/ppermute | solution.py:56
  63.6 84.1 %collective-permute-start.10 = (bf16[40,4096]{1,0:T(8,128)(2,1)S(1)}, bf16[40,4096]{1,0:T(8,128)(2,1)}, u32[]{:S(2)}, u32[]{:S(2)}) collective-permute-start(bf16[40,4096]{1,0:T(8,128)(2,1)S(1)} %get-tuple-element.92), channel_id=1, source_target_pairs={{0,2},{1,3},{2,0},{3,1},{4,6},{5,7},{6,4},{7,5},{8,10},{9,11},{10,... | collective-permute-start | bytes 983048 | tf_op jit(solution)/shard_map/ppermute | solution.py:56
  64.5 84.7 %collective-permute-start.11 = (bf16[40,4096]{1,0:T(8,128)(2,1)S(1)}, bf16[40,4096]{1,0:T(8,128)(2,1)S(1)}, u32[]{:S(2)}, u32[]{:S(2)}) collective-permute-start(bf16[40,4096]{1,0:T(8,128)(2,1)S(1)} %get-tuple-element.92), channel_id=1, source_target_pairs={{0,3},{1,0},{2,1},{3,2},{4,7},{5,4},{6,5},{7,6},{8,11},{9,8},{10,9... | collective-permute-start | bytes 983048 | tf_op jit(solution)/shard_map/ppermute | solution.py:56
  66.0 83.5 %collective-permute-start = (bf16[128,1536]{1,0:T(8,128)(2,1)S(1)}, bf16[128,1536]{1,0:T(8,128)(2,1)S(1)}, u32[]{:S(2)}, u32[]{:S(2)}) collective-permute-start(bf16[128,1536]{1,0:T(8,128)(2,1)S(1)} %copy-done.12), channel_id=1, source_target_pairs={{0,1},{1,2},{2,3},{3,0},{4,5},{5,6},{6,7},{7,4},{8,9},{9,10},{10,1... | collective-permute-start | bytes 1179656 | tf_op jit(solution)/shard_map/ppermute | solution.py:56
  66.6 86.3 %collective-permute-start.1 = (bf16[128,1536]{1,0:T(8,128)(2,1)S(1)}, bf16[128,1536]{1,0:T(8,128)(2,1)S(1)}, u32[]{:S(2)}, u32[]{:S(2)}) collective-permute-start(bf16[128,1536]{1,0:T(8,128)(2,1)S(1)} %copy-done.12), channel_id=1, source_target_pairs={{0,2},{1,3},{2,0},{3,1},{4,6},{5,7},{6,4},{7,5},{8,10},{9,11},{10,... | collective-permute-start | bytes 1179656 | tf_op jit(solution)/shard_map/ppermute | solution.py:56
  147.7 60.3 %collective-permute-start.6 = (s32[128,3]{0,1:T(4,128)}, s32[128,3]{0,1:T(4,128)}, u32[]{:S(2)}, u32[]{:S(2)}) collective-permute-start(s32[128,3]{0,1:T(4,128)} %param.31), channel_id=1, source_target_pairs={{0,1},{1,2},{2,3},{3,0},{4,5},{5,6},{6,7},{7,4},{8,9},{9,10},{10,1... | collective-permute-start | bytes 4616 | tf_op jit(solution)/shard_map/ppermute | solution.py:56
  149.3 59.4 %collective-permute-start.7 = (s32[128,3]{0,1:T(4,128)}, s32[128,3]{0,1:T(4,128)}, u32[]{:S(2)}, u32[]{:S(2)}) collective-permute-start(s32[128,3]{0,1:T(4,128)} %param.31), channel_id=1, source_target_pairs={{0,2},{1,3},{2,0},{3,1},{4,6},{5,7},{6,4},{7,5},{8,10},{9,11},{10,... | collective-permute-start | bytes 4616 | tf_op jit(solution)/shard_map/ppermute | solution.py:56
  149.5 59.9 %collective-permute-start.8 = (s32[128,3]{0,1:T(4,128)}, s32[128,3]{0,1:T(4,128)}, u32[]{:S(2)}, u32[]{:S(2)}) collective-permute-start(s32[128,3]{0,1:T(4,128)} %param.31), channel_id=1, source_target_pairs={{0,3},{1,0},{2,1},{3,2},{4,7},{5,4},{6,5},{7,6},{8,11},{9,8},{10,9... | collective-permute-start | bytes 4616 | tf_op jit(solution)/shard_map/ppermute | solution.py:56
  203.8 73.9 %all-gather.11.cloned.1.call-start = ((), (), s32[]{:S(2)}) async-start(), calls=%async_computation.9 | async-start | bytes 7077888 | tf_op jit(solution)/shard_map/all_gather | solution.py:508
  214.0 90.2 %all-gather.17.cloned.1.call-start = ((), (), s32[]{:S(2)}) async-start(), calls=%async_computation.12 | async-start | bytes 1327104 | tf_op jit(solution)/shard_map/all_gather | solution.py:409
  215.4 161.7 %all-gather.19.cloned.1.call-start = ((), (), s32[]{:S(2)}) async-start(), calls=%async_computation.13 | async-start | bytes 7077888 | tf_op jit(solution)/shard_map/all_gather | solution.py:412
  245.1 141.6 %all-gather.21.cloned.1.call-start = ((), (), s32[]{:S(2)}) async-start(), calls=%async_computation.14 | async-start | bytes 3538944 | tf_op jit(solution)/shard_map/all_gather | solution.py:416
  245.7 384.4 %reduce-scatter.10.cloned.1.call-start = ((), (), s32[]{:S(2)}) async-start(), calls=%async_computation.16 | async-start | bytes 2211840 | tf_op jit(solution)/shard_map/reduce_scatter | solution.py:563
  308.1 28.6 %collective-permute-start.17 = (bf16[128,1536]{1,0:T(8,128)(2,1)S(1)}, bf16[128,1536]{1,0:T(8,128)(2,1)S(1)}, u32[]{:S(2)}, u32[]{:S(2)}) collective-permute-start(bf16[128,1536]{1,0:T(8,128)(2,1)S(1)} %get-tuple-element.114), channel_id=1, source_target_pairs={{0,2},{1,3},{2,0},{3,1},{4,6},{5,7},{6,4},{7,5},{8,10},{9,11},{10,... | collective-permute-start | bytes 1179656 | tf_op jit(solution)/shard_map/ppermute | solution.py:80
  310.5 26.1 %collective-permute-start.18 = (bf16[128,1536]{1,0:T(8,128)(2,1)S(1)}, bf16[128,1536]{1,0:T(8,128)(2,1)S(1)}, u32[]{:S(2)}, u32[]{:S(2)}) collective-permute-start(bf16[128,1536]{1,0:T(8,128)(2,1)S(1)} %get-tuple-element.113), channel_id=1, source_target_pairs={{0,3},{1,0},{2,1},{3,2},{4,7},{5,4},{6,5},{7,6},{8,11},{9,8},{10,9... | collective-permute-start | bytes 1179656 | tf_op jit(solution)/shard_map/ppermute | solution.py:80
  340.0 19.9 %collective-permute-start.19 = (bf16[128,1536]{1,0:T(8,128)(2,1)S(1)}, bf16[128,1536]{1,0:T(8,128)(2,1)S(1)}, u32[]{:S(2)}, u32[]{:S(2)}) collective-permute-start(bf16[128,1536]{1,0:T(8,128)(2,1)S(1)} %get-tuple-element.86), channel_id=1, source_target_pairs={{0,1},{1,2},{2,3},{3,0},{4,5},{5,6},{6,7},{7,4},{8,9},{9,10},{10,1... | collective-permute-start | bytes 1179656 | tf_op jit(solution)/shard_map/ppermute | solution.py:56
  349.0 26.5 %collective-permute-start.20 = (bf16[128,1536]{1,0:T(8,128)(2,1)S(1)}, bf16[128,1536]{1,0:T(8,128)(2,1)S(1)}, u32[]{:S(2)}, u32[]{:S(2)}) collective-permute-start(bf16[128,1536]{1,0:T(8,128)(2,1)S(1)} %get-tuple-element.86), channel_id=1, source_target_pairs={{0,2},{1,3},{2,0},{3,1},{4,6},{5,7},{6,4},{7,5},{8,10},{9,11},{10,... | collective-permute-start | bytes 1179656 | tf_op jit(solution)/shard_map/ppermute | solution.py:56
  350.4 25.8 %collective-permute-start.21 = (bf16[128,1536]{1,0:T(8,128)(2,1)S(1)}, bf16[128,1536]{1,0:T(8,128)(2,1)S(1)}, u32[]{:S(2)}, u32[]{:S(2)}) collective-permute-start(bf16[128,1536]{1,0:T(8,128)(2,1)S(1)} %get-tuple-element.86), channel_id=1, source_target_pairs={{0,3},{1,0},{2,1},{3,2},{4,7},{5,4},{6,5},{7,6},{8,11},{9,8},{10,9... | collective-permute-start | bytes 1179656 | tf_op jit(solution)/shard_map/ppermute | solution.py:56
  390.9 20.7 %collective-permute-start.25 = (bf16[128,1536]{1,0:T(8,128)(2,1)S(1)}, bf16[128,1536]{1,0:T(8,128)(2,1)S(1)}, u32[]{:S(2)}, u32[]{:S(2)}) collective-permute-start(bf16[128,1536]{1,0:T(8,128)(2,1)S(1)} %get-tuple-element.109), channel_id=1, source_target_pairs={{0,1},{1,2},{2,3},{3,0},{4,5},{5,6},{6,7},{7,4},{8,9},{9,10},{10,1... | collective-permute-start | bytes 1179656 | tf_op jit(solution)/shard_map/ppermute | solution.py:80
  399.1 28.2 %collective-permute-start.26 = (bf16[128,1536]{1,0:T(8,128)(2,1)S(1)}, bf16[128,1536]{1,0:T(8,128)(2,1)S(1)}, u32[]{:S(2)}, u32[]{:S(2)}) collective-permute-start(bf16[128,1536]{1,0:T(8,128)(2,1)S(1)} %get-tuple-element.111), channel_id=1, source_target_pairs={{0,2},{1,3},{2,0},{3,1},{4,6},{5,7},{6,4},{7,5},{8,10},{9,11},{10,... | collective-permute-start | bytes 1179656 | tf_op jit(solution)/shard_map/ppermute | solution.py:80
  402.0 25.3 %collective-permute-start.27 = (bf16[128,1536]{1,0:T(8,128)(2,1)S(1)}, bf16[128,1536]{1,0:T(8,128)(2,1)S(1)}, u32[]{:S(2)}, u32[]{:S(2)}) collective-permute-start(bf16[128,1536]{1,0:T(8,128)(2,1)S(1)} %get-tuple-element.110), channel_id=1, source_target_pairs={{0,3},{1,0},{2,1},{3,2},{4,7},{5,4},{6,5},{7,6},{8,11},{9,8},{10,9... | collective-permute-start | bytes 1179656 | tf_op jit(solution)/shard_map/ppermute | solution.py:80
  430.3 19.0 %collective-permute-start.28 = (bf16[128,1536]{1,0:T(8,128)(2,1)S(1)}, bf16[128,1536]{1,0:T(8,128)(2,1)S(1)}, u32[]{:S(2)}, u32[]{:S(2)}) collective-permute-start(bf16[128,1536]{1,0:T(8,128)(2,1)S(1)} %get-tuple-element.82), channel_id=1, source_target_pairs={{0,1},{1,2},{2,3},{3,0},{4,5},{5,6},{6,7},{7,4},{8,9},{9,10},{10,1... | collective-permute-start | bytes 1179656 | tf_op jit(solution)/shard_map/ppermute | solution.py:56
  439.3 25.7 %collective-permute-start.29 = (bf16[128,1536]{1,0:T(8,128)(2,1)S(1)}, bf16[128,1536]{1,0:T(8,128)(2,1)S(1)}, u32[]{:S(2)}, u32[]{:S(2)}) collective-permute-start(bf16[128,1536]{1,0:T(8,128)(2,1)S(1)} %get-tuple-element.82), channel_id=1, source_target_pairs={{0,2},{1,3},{2,0},{3,1},{4,6},{5,7},{6,4},{7,5},{8,10},{9,11},{10,... | collective-permute-start | bytes 1179656 | tf_op jit(solution)/shard_map/ppermute | solution.py:56
  439.7 25.3 %collective-permute-start.30 = (bf16[128,1536]{1,0:T(8,128)(2,1)S(1)}, bf16[128,1536]{1,0:T(8,128)(2,1)S(1)}, u32[]{:S(2)}, u32[]{:S(2)}) collective-permute-start(bf16[128,1536]{1,0:T(8,128)(2,1)S(1)} %get-tuple-element.82), channel_id=1, source_target_pairs={{0,3},{1,0},{2,1},{3,2},{4,7},{5,4},{6,5},{7,6},{8,11},{9,8},{10,9... | collective-permute-start | bytes 1179656 | tf_op jit(solution)/shard_map/ppermute | solution.py:56
  472.0 21.4 %collective-permute-start.31 = (bf16[128,1536]{1,0:T(8,128)(2,1)S(1)}, bf16[128,1536]{1,0:T(8,128)(2,1)S(1)}, u32[]{:S(2)}, u32[]{:S(2)}) collective-permute-start(bf16[128,1536]{1,0:T(8,128)(2,1)S(1)} %get-tuple-element.106), channel_id=1, source_target_pairs={{0,1},{1,2},{2,3},{3,0},{4,5},{5,6},{6,7},{7,4},{8,9},{9,10},{10,1... | collective-permute-start | bytes 1179656 | tf_op jit(solution)/shard_map/ppermute | solution.py:80
  480.9 28.1 %collective-permute-start.32 = (bf16[128,1536]{1,0:T(8,128)(2,1)S(1)}, bf16[128,1536]{1,0:T(8,128)(2,1)S(1)}, u32[]{:S(2)}, u32[]{:S(2)}) collective-permute-start(bf16[128,1536]{1,0:T(8,128)(2,1)S(1)} %get-tuple-element.108), channel_id=1, source_target_pairs={{0,2},{1,3},{2,0},{3,1},{4,6},{5,7},{6,4},{7,5},{8,10},{9,11},{10,... | collective-permute-start | bytes 1179656 | tf_op jit(solution)/shard_map/ppermute | solution.py:80
  483.9 25.1 %collective-permute-start.33 = (bf16[128,1536]{1,0:T(8,128)(2,1)S(1)}, bf16[128,1536]{1,0:T(8,128)(2,1)S(1)}, u32[]{:S(2)}, u32[]{:S(2)}) collective-permute-start(bf16[128,1536]{1,0:T(8,128)(2,1)S(1)} %get-tuple-element.107), channel_id=1, source_target_pairs={{0,3},{1,0},{2,1},{3,2},{4,7},{5,4},{6,5},{7,6},{8,11},{9,8},{10,9... | collective-permute-start | bytes 1179656 | tf_op jit(solution)/shard_map/ppermute | solution.py:80
  514.1 19.0 %collective-permute-start.34 = (bf16[128,1536]{1,0:T(8,128)(2,1)S(1)}, bf16[128,1536]{1,0:T(8,128)(2,1)S(1)}, u32[]{:S(2)}, u32[]{:S(2)}) collective-permute-start(bf16[128,1536]{1,0:T(8,128)(2,1)S(1)} %get-tuple-element.80), channel_id=1, source_target_pairs={{0,1},{1,2},{2,3},{3,0},{4,5},{5,6},{6,7},{7,4},{8,9},{9,10},{10,1... | collective-permute-start | bytes 1179656 | tf_op jit(solution)/shard_map/ppermute | solution.py:56
  523.0 25.7 %collective-permute-start.35 = (bf16[128,1536]{1,0:T(8,128)(2,1)S(1)}, bf16[128,1536]{1,0:T(8,128)(2,1)S(1)}, u32[]{:S(2)}, u32[]{:S(2)}) collective-permute-start(bf16[128,1536]{1,0:T(8,128)(2,1)S(1)} %get-tuple-element.80), channel_id=1, source_target_pairs={{0,2},{1,3},{2,0},{3,1},{4,6},{5,7},{6,4},{7,5},{8,10},{9,11},{10,... | collective-permute-start | bytes 1179656 | tf_op jit(solution)/shard_map/ppermute | solution.py:56
  523.5 25.2 %collective-permute-start.36 = (bf16[128,1536]{1,0:T(8,128)(2,1)S(1)}, bf16[128,1536]{1,0:T(8,128)(2,1)S(1)}, u32[]{:S(2)}, u32[]{:S(2)}) collective-permute-start(bf16[128,1536]{1,0:T(8,128)(2,1)S(1)} %get-tuple-element.80), channel_id=1, source_target_pairs={{0,3},{1,0},{2,1},{3,2},{4,7},{5,4},{6,5},{7,6},{8,11},{9,8},{10,9... | collective-permute-start | bytes 1179656 | tf_op jit(solution)/shard_map/ppermute | solution.py:56
  563.4 136.8 %reduce-scatter.8.cloned.1.call-start = ((), (), s32[]{:S(2)}) async-start(), calls=%async_computation.15 | async-start | bytes 7077888 | tf_op jit(solution)/shard_map/reduce_scatter | solution.py:563
  594.0 298.0 %reduce-scatter.18.cloned.1.call-start = ((), (), s32[]{:S(2)}) async-start(), calls=%async_computation.21 | async-start | bytes 7077888 | tf_op jit(solution)/shard_map/reduce_scatter | solution.py:563
  602.5 304.9 %reduce-scatter.14.cloned.1.call-start = ((), (), s32[]{:S(2)}) async-start(), calls=%async_computation.19 | async-start | bytes 1327104 | tf_op jit(solution)/shard_map/reduce_scatter | solution.py:563
  605.9 303.8 %reduce-scatter.20.cloned.1.call-start = ((), (), s32[]{:S(2)}) async-start(), calls=%async_computation.22 | async-start | bytes 3538944 | tf_op jit(solution)/shard_map/reduce_scatter | solution.py:563
  611.3 361.2 %reduce-scatter.12.cloned.1.call-start = ((), (), s32[]{:S(2)}) async-start(), calls=%async_computation.18 | async-start | bytes 3981312 | tf_op jit(solution)/shard_map/reduce_scatter | solution.py:563
  747.3 236.2 %all-gather.23.cloned.1.call-start = ((), (), s32[]{:S(2)}) async-start(), calls=%async_computation.17 | async-start | bytes 2949120 | tf_op jit(solution)/shard_map/all_gather | solution.py:594
  754.1 27.8 %collective-permute-start.38 = (bf16[128,1536]{1,0:T(8,128)(2,1)S(1)}, bf16[128,1536]{1,0:T(8,128)(2,1)S(1)}, u32[]{:S(2)}, u32[]{:S(2)}) collective-permute-start(bf16[128,1536]{1,0:T(8,128)(2,1)S(1)} %get-tuple-element.105), channel_id=1, source_target_pairs={{0,2},{1,3},{2,0},{3,1},{4,6},{5,7},{6,4},{7,5},{8,10},{9,11},{10,... | collective-permute-start | bytes 1179656 | tf_op jit(solution)/shard_map/ppermute | solution.py:80
  754.4 27.5 %collective-permute-start.39 = (bf16[128,1536]{1,0:T(8,128)(2,1)S(1)}, bf16[128,1536]{1,0:T(8,128)(2,1)S(1)}, u32[]{:S(2)}, u32[]{:S(2)}) collective-permute-start(bf16[128,1536]{1,0:T(8,128)(2,1)S(1)} %get-tuple-element.104), channel_id=1, source_target_pairs={{0,3},{1,0},{2,1},{3,2},{4,7},{5,4},{6,5},{7,6},{8,11},{9,8},{10,9... | collective-permute-start | bytes 1179656 | tf_op jit(solution)/shard_map/ppermute | solution.py:80
  865.3 19.9 %collective-permute-start.41 = (bf16[40,4096]{1,0:T(8,128)(2,1)S(1)}, bf16[40,4096]{1,0:T(8,128)(2,1)S(1)}, u32[]{:S(2)}, u32[]{:S(2)}) collective-permute-start(bf16[40,4096]{1,0:T(8,128)(2,1)S(1)} %get-tuple-element.117), channel_id=1, source_target_pairs={{0,2},{1,3},{2,0},{3,1},{4,6},{5,7},{6,4},{7,5},{8,10},{9,11},{10,... | collective-permute-start | bytes 983048 | tf_op jit(solution)/shard_map/ppermute | solution.py:80
  866.4 18.8 %collective-permute-start.42 = (bf16[40,4096]{1,0:T(8,128)(2,1)S(1)}, bf16[40,4096]{1,0:T(8,128)(2,1)S(1)}, u32[]{:S(2)}, u32[]{:S(2)}) collective-permute-start(bf16[40,4096]{1,0:T(8,128)(2,1)S(1)} %get-tuple-element.116), channel_id=1, source_target_pairs={{0,3},{1,0},{2,1},{3,2},{4,7},{5,4},{6,5},{7,6},{8,11},{9,8},{10,9... | collective-permute-start | bytes 983048 | tf_op jit(solution)/shard_map/ppermute | solution.py:80
  886.1 118.4 %reduce-scatter.16.cloned.1.call-start = ((), (), s32[]{:S(2)}) async-start(), calls=%async_computation.20 | async-start | bytes 7077888 | tf_op jit(solution)/shard_map/reduce_scatter | solution.py:563
  905.5 17.2 %collective-permute-start.51 = (bf16[1,48,2048]{2,1,0:T(8,128)(2,1)}, bf16[1,48,2048]{2,1,0:T(8,128)(2,1)}, u32[]{:S(2)}, u32[]{:S(2)}) collective-permute-start(bf16[1,48,2048]{2,1,0:T(8,128)(2,1)} %get-tuple-element.124), channel_id=1, source_target_pairs={{0,2},{1,3},{2,0},{3,1},{4,6},{5,7},{6,4},{7,5},{8,10},{9,11},{10,... | collective-permute-start | bytes 589832 | tf_op jit(solution)/shard_map/ppermute | solution.py:67
  988.3 18.8 %collective-permute-start.45 = (bf16[1,48,1152]{2,1,0:T(8,128)(2,1)S(1)}, bf16[1,48,1152]{2,1,0:T(8,128)(2,1)S(1)}, u32[]{:S(2)}, u32[]{:S(2)}) collective-permute-start(bf16[1,48,1152]{2,1,0:T(8,128)(2,1)S(1)} %get-tuple-element.149), channel_id=1, source_target_pairs={{0,3},{1,0},{2,1},{3,2},{4,7},{5,4},{6,5},{7,6},{8,11},{9,8},{10,9... | collective-permute-start | bytes 331784 | tf_op jit(solution)/shard_map/ppermute | solution.py:67
  (134 other events, 1440.2 us)
Sparse Core Ops, SparseCore 0:
  20.7 154.7 all-reduce.6
Sparse Core Ops, SparseCore 1:
  36.3 37.8 all-gather.8
  76.5 45.3 all-gather.12
  203.9 25.8 all-gather.14
  232.3 45.4 all-gather.10
  280.3 23.8 all-gather.16
  306.6 45.3 all-gather.18
  353.7 32.0 all-gather.20
  563.5 66.6 reduce-scatter.9
  633.4 66.7 reduce-scatter.7
  703.6 61.6 reduce-scatter.17
  768.3 36.7 reduce-scatter.13
  808.5 46.2 reduce-scatter.19
  858.7 47.8 reduce-scatter.11
  909.0 30.5 all-gather.22
  942.9 61.5 reduce-scatter.15
